TPU v7x, 32 devices: a whole 2x2x4 slice. The times are simulated.
32 devices in a mesh: groups: 2 (over x), wide: 16 (over z, y, core).
Axes of the slice: x: 2, y: 2, z: 4, core: 2. Of those that a mesh axis runs over, the one named last changes fastest.
Arguments:
- fine_field: float32 [256, 64, 512], P(None, ('groups', 'wide')), parts along dimension 1, may hold values from -6 to 6
- w_down_fine: float32 [8, 256, 512], replicated, may hold values from -0.125 to 0.125
- w_conv_mid: float32 [27, 512, 512], P(None, 'wide'), may hold values from -0.0546875 to 0.0546875
- w_down_mid: float32 [8, 512, 1024], P(None, 'wide'), may hold values from -0.09375 to 0.09375
- w_conv_deep: float32 [27, 1024, 1024], P(None, 'wide'), may hold values from -0.0390625 to 0.0390625
- w_up_deep: float32 [8, 1024, 512], P(None, 'wide'), may hold values from -0.1875 to 0.1875
- w_up_mid: float32 [8, 512, 256], replicated, may hold values from -0.25 to 0.25
Outputs:
- fine_update: float32 [256, 64, 512], P(None, ('groups', 'wide')), parts along dimension 1
There are 2 independent parts, one for each index of `groups`. A program takes and returns all parts, laid end to end along the dimension named above; an argument that names none is the same for every part. Nothing has to cross between parts.
All inputs are finite; a program needn't handle non-finite values.
Results may differ from a plain program's by a relative error of at most 0.0001.
Values sent between devices are 32-bit elements; how exact they have to be, the bound alone decides.
No kernel may reach another device: no remote copies, remote signals or barrier semaphores. Data moves between devices by JAX's collectives and lax.ppermute only.
A program may use at most 192 MiB of HBM per device.

v0:
```python
import jax
import jax.numpy as jnp
from jax import lax
from jax.sharding import PartitionSpec as P

YA = 32
ZA = 16


HIGHEST_MODE = lax.Precision.HIGHEST


def selector(rows, cols, b, c):
    big_cells = jnp.arange(rows * cols)[:, None]
    small_cells = jnp.arange(rows // 2 * (cols // 2))[None, :]
    target = (2 * (small_cells // (cols // 2)) + b) * cols + 2 * (small_cells % (cols // 2)) + c
    return (big_cells == target).astype(jnp.float32)


def valid_mask(cells, rows, cols, step_row, step_col):
    places = jnp.arange(cells)
    row_of = places // cols % rows + step_row
    col_of = places % cols + step_col
    inside = (row_of >= 0) & (row_of < rows) & (col_of >= 0) & (col_of < cols)
    return inside.astype(jnp.float32)


def shift_flat(field, offset, weights_mask):
    width = abs(offset)
    last = field.ndim - 1
    padded = jnp.pad(field, [(0, 0)] * last + [(width, width)])
    cells = field.shape[last]
    shifted = lax.slice_in_dim(padded, width + offset, width + offset + cells, axis=last)
    return shifted * weights_mask


def lift_apply(weights, source, row_count, mid_rows, mid_cols, deep_planes, deep_rows, deep_cols):
    mid_planes = 2 * deep_planes
    mid_cells = mid_rows * mid_cols
    spread = jnp.einsum("tco,cn->ton", weights, source, precision=HIGHEST_MODE)
    summed = jnp.zeros((2, row_count, deep_planes, mid_cells), jnp.float32)
    for b in range(2):
        for c in range(2):
            paired = jnp.stack([spread[2 * b + c], spread[4 + 2 * b + c]])
            paired = paired.reshape(2, row_count, deep_planes, deep_rows * deep_cols)
            summed = summed + jnp.dot(
                paired, selector(mid_rows, mid_cols, b, c).T, precision=HIGHEST_MODE
            )
    return summed.transpose(1, 2, 0, 3).reshape(row_count, mid_planes, mid_cells)


def shards(fine_field, w_down_fine, w_conv_mid, w_down_mid, w_conv_deep, w_up_deep, w_up_mid):
    wide_count = lax.axis_size("wide")
    mid_rows, mid_cols = (YA // 2, ZA // 2)
    deep_rows, deep_cols = (YA // 4, ZA // 4)
    mid_cells = mid_rows * mid_cols
    deep_planes = wide_count // 2
    deep_cells = deep_planes * deep_rows * deep_cols
    chan_fine = fine_field.shape[0]
    chan_mid = w_down_fine.shape[2]
    chan_deep = w_down_mid.shape[2]
    mid_local = w_conv_mid.shape[1]
    deep_local = w_conv_deep.shape[1]
    fine_picks = [None] * 8
    for b in range(2):
        for c in range(2):
            reduced = jnp.dot(fine_field, selector(YA, ZA, b, c), precision=HIGHEST_MODE)
            for a in range(2):
                fine_picks[4 * a + 2 * b + c] = reduced[:, a, :]
    mid_input = jnp.einsum(
        "tco,tcn->on", w_down_fine, jnp.stack(fine_picks), precision=HIGHEST_MODE
    )[:, None, :]
    mid_kernel = w_conv_mid.reshape(3, 3, 3, mid_local, chan_mid)
    mid_start = jnp.zeros((mid_local, wide_count + 2, mid_cells), jnp.float32)
    running = mid_start
    shard_piece = lax.all_gather(mid_input, "wide", axis=1, tiled=True)
    first_row = jnp.int32(0)
    row_count = shard_piece.shape[1]
    summed = jnp.zeros((3, mid_local, row_count, mid_cells), jnp.float32)
    for convolve_b in range(3):
        for convolve_c in range(3):
            shifted = shift_flat(
                shard_piece,
                (convolve_b - 1) * mid_cols + (convolve_c - 1),
                valid_mask(mid_cells, mid_rows, mid_cols, convolve_b - 1, convolve_c - 1),
            )
            summed = summed + jnp.einsum(
                "aoc,ckn->aokn",
                mid_kernel[:, convolve_b, convolve_c],
                shifted,
                precision=HIGHEST_MODE,
            )
    for convolve_a in range(3):
        offset_row = first_row - convolve_a + 2
        current = lax.dynamic_slice_in_dim(running, offset_row, row_count, 1)
        running = lax.dynamic_update_slice_in_dim(
            running, current + summed[convolve_a], offset_row, 1
        )
    folded = running
    mid_field = jax.nn.relu(folded[:, 1:-1])
    deep_picks = [None] * 8
    for b in range(2):
        for c in range(2):
            reduced = jnp.dot(mid_field, selector(mid_rows, mid_cols, b, c), precision=HIGHEST_MODE)
            reduced = reduced.reshape(mid_local, deep_planes, 2, deep_rows * deep_cols)
            for a in range(2):
                deep_picks[4 * a + 2 * b + c] = reduced[:, :, a, :].reshape(mid_local, deep_cells)
    deep_stack = jnp.stack(deep_picks)
    deep_kernel = w_conv_deep.reshape(3, 3, 3, deep_local, chan_deep)

    def convolve_deep(running, shard_piece):
        row_count = shard_piece.shape[0]
        for a in range(3):
            shifted_list = []
            for b in range(3):
                for c in range(3):
                    offset = (a - 1) * deep_rows * deep_cols + (b - 1) * deep_cols + (c - 1)
                    shifted_list.append(
                        shift_flat(
                            shard_piece,
                            offset,
                            valid_mask(deep_cells, deep_rows, deep_cols, b - 1, c - 1),
                        )
                    )
            shifted = jnp.stack(shifted_list)
            running = running + jnp.einsum(
                "tok,tkn->on",
                deep_kernel[a].reshape(9, deep_local, row_count),
                shifted,
                precision=HIGHEST_MODE,
            )
        return running

    deep_start = jnp.zeros((deep_local, deep_cells), jnp.float32)
    deep_part = jax.nn.relu(
        lax.psum_scatter(
            jnp.einsum("tco,tcn->on", w_down_mid, deep_stack, precision=HIGHEST_MODE),
            "wide",
            scatter_dimension=0,
            tiled=True,
        )
    )
    deep_output = jax.nn.relu(
        convolve_deep(deep_start, lax.all_gather(deep_part, "wide", axis=0, tiled=True))
    )
    deep_every = lax.all_gather(deep_output, "wide", axis=0, tiled=True)
    w_columns = lax.all_to_all(w_up_deep, "wide", split_axis=2, concat_axis=1, tiled=True)
    lifted = lift_apply(
        w_columns, deep_every, mid_local, mid_rows, mid_cols, deep_planes, deep_rows, deep_cols
    )
    mid_merged = jax.nn.relu(mid_field + lifted)
    merged_every = lax.all_gather(mid_merged, "wide", axis=0, tiled=True)
    mid_plane = lax.dynamic_slice_in_dim(merged_every, lax.axis_index("wide"), 1, 1)
    spread_fine = jnp.einsum("tco,cn->ton", w_up_mid, mid_plane[:, 0, :], precision=HIGHEST_MODE)
    fine_sum = jnp.zeros((2, chan_fine, YA * ZA), jnp.float32)
    for b in range(2):
        for c in range(2):
            paired = jnp.stack([spread_fine[2 * b + c], spread_fine[4 + 2 * b + c]])
            fine_sum = fine_sum + jnp.dot(paired, selector(YA, ZA, b, c).T, precision=HIGHEST_MODE)
    return fine_sum.transpose(1, 0, 2)


def solution(mesh):
    return jax.shard_map(
        shards,
        mesh=mesh,
        in_specs=(
            P(None, ("groups", "wide"), None),
            P(),
            P(None, "wide", None),
            P(None, "wide", None),
            P(None, "wide", None),
            P(None, "wide", None),
            P(),
        ),
        out_specs=P(None, ("groups", "wide"), None),
        check_vma=False,
    )
```

profile of v0, /device:TPU:0, one launch (start us, length us, event | category | flops | bytes accessed | tf_op | source)
XLA Modules:
  0.0 353.2 jit_solution(16231777582741179263)
XLA Ops:
  11.1 3.1 convolution_bitcast_fusion.2
  14.5 53.0 %all-gather.12.cloned.1.call-done = f32[512,2048]{0,1:T(8,128)} async-done(((f32[512,128]{0,1:T(8,128)}), f32[512,2048]{0,1:T(8,128)}) %all-gather.12.cloned.1.call-update) | async-done | bytes 4194320 | tf_op jit(solution)/shard_map/all_gather | solution.py:76
  67.5 5.6 %copy.118 = f32[512,16,128]{2,0,1:T(8,128)} copy(f32[512,16,128]{0,2,1:T(8,128)} %bitcast.430) | data formatting | bytes 8388608 | tf_op jit(solution)/shard_map/all_gather | solution.py:76
  73.2 5.4 %fusion.2 = f32[16,128,3,32]{1,3,2,0:T(8,128)S(1)} fusion(f32[512,16,128]{2,0,1:T(8,128)} %copy.118, f32[128]{0:T(128)S(1)} %and_convert_fusion.17, f32[3,3,3,32,512]{4,3,2,1,0:T(8,128)S(1)} %bitcast.431), kind=kOutput, calls=%fused_computation.10 | convolution fusion | flops 1209008128 | bytes 5177856 | tf_op jit(solution)/shard_map/aoc,ckn->aokn/dot_general | solution.py:87
  78.6 2.8 fusion.32
  81.4 3.1 fusion.66
  84.5 3.1 fusion.60
  87.5 3.3 fusion.75
  90.8 3.1 fusion.51
  93.8 3.1 fusion.57
  96.9 3.1 fusion.63
  100.0 3.5 fusion.72
  112.7 56.2 %reduce-scatter.4.cloned.1.call-done = f32[64,256]{1,0:T(8,128)} async-done(((f32[1024,256]{1,0:T(8,128)}), f32[64,256]{1,0:T(8,128)}) %reduce-scatter.4.cloned.1.call-update) | async-done | bytes 65552 | tf_op jit(solution)/shard_map/reduce_scatter | solution.py:136
  173.5 3.7 %all-to-all-start = ((f32[16,1,16384]{2,1,0:T(1,128)}), f32[16,1,16384]{2,1,0:T(1,128)S(1)}, u32[]{:S(2)}, u32[]{:S(2)}) async-start(f32[16,1,16384]{2,1,0:T(1,128)} %reshape.464), calls=%async_computation | async-start | bytes 2097152 | tf_op jit(solution)/shard_map/all_to_all | solution.py:147
  177.5 35.6 %all-gather.6.cloned.1.call-done = f32[1024,256]{1,0:T(8,128)} async-done(((f32[64,256]{1,0:T(8,128)}), f32[1024,256]{1,0:T(8,128)}) %all-gather.6.cloned.1.call-update) | async-done | bytes 1048592 | tf_op jit(solution)/shard_map/all_gather | solution.py:144
  213.1 3.0 fusion.102
  222.9 7.3 %fusion.94 = f32[256,64]{0,1:T(8,128)S(1)} fusion(f32[9,1024,256]{2,1,0:T(8,128)S(1)} %get-tuple-element.15, f32[27,64,1024]{2,1,0:T(8,128)} %param.11), kind=kOutput, calls=%fused_computation.105 | convolution fusion | flops 1811939328 | bytes 11862016 | tf_op jit(solution)/shard_map/tok,tkn->on/dot_general | solution.py:126
  230.2 7.5 %fusion.97 = f32[256,64]{0,1:T(8,128)S(1)} fusion(f32[9,1024,256]{2,1,0:T(8,128)S(1)} %get-tuple-element.14, f32[27,64,1024]{2,1,0:T(8,128)} %param.11), kind=kOutput, calls=%fused_computation.106 | convolution fusion | flops 1811939328 | bytes 11862016 | tf_op jit(solution)/shard_map/tok,tkn->on/dot_general | solution.py:126
  237.7 7.9 %fusion.91 = f32[64,256]{1,0:T(8,128)} fusion(f32[256,64]{0,1:T(8,128)S(1)} %fusion.97, f32[256,64]{0,1:T(8,128)S(1)} %fusion.94, f32[9,1024,256]{2,1,0:T(8,128)S(1)} %get-tuple-element.13, f32[27,64,1024]{2,1,0:T(8,128)} %param.11), kind=kOutput, calls=%fused_computation.104 | convolution fusion | flops 1811988480 | bytes 11993088 | tf_op jit(solution)/shard_map/tok,tkn->on/dot_general | solution.py:126
  246.5 3.2 reduce.32
  250.5 2.5 copy.141
  255.0 27.6 %all-gather.8.cloned.1.call-done = f32[1024,256]{1,0:T(8,128)} async-done(((f32[64,256]{1,0:T(8,128)}), f32[1024,256]{1,0:T(8,128)}) %all-gather.8.cloned.1.call-update) | async-done | bytes 1048592 | tf_op jit(solution)/shard_map/all_gather | solution.py:146
  287.6 49.5 %all-gather.10.cloned.1.call-done = f32[512,16,128]{2,0,1:T(8,128)} async-done(((f32[32,16,128]{2,0,1:T(8,128)}), f32[512,16,128]{2,0,1:T(8,128)}) %all-gather.10.cloned.1.call-update) | async-done | bytes 4194320 | tf_op jit(solution)/shard_map/all_gather | solution.py:152
  337.2 4.6 %convolution_bitcast_fusion = f32[8,256,128]{1,2,0:T(8,128)S(1)} fusion(f32[8,512,256]{2,1,0:T(8,128)} %param.13, f32[512,16,128]{2,0,1:T(8,128)} %all-gather.10.cloned.1.call-done, s32[]{:T(128)S(6)} %select_n.760), kind=kOutput, calls=%fused_computation.76 | convolution fusion | flops 1610612736 | bytes 5505028 | tf_op jit(solution)/shard_map/tco,cn->ton/dot_general | solution.py:154
  (124 shorter events, 38.2 us)
Async XLA Ops:
  6.5 1.2 copy-start
  6.5 61.0 %all-gather.12.cloned.1.call-start = ((), (), s32[]{:S(2)}) async-start(), calls=%async_computation.5 | async-start | bytes 4456448 | tf_op jit(solution)/shard_map/all_gather | solution.py:76
  6.5 4.6 %copy-start.4 = (f32[8,256,512]{2,1,0:T(8,128)S(1)}, f32[8,256,512]{2,1,0:T(8,128)}, u32[]{:S(2)}) copy-start(f32[8,256,512]{2,1,0:T(8,128)} %param.8) | copy-start | bytes 12582916
  14.3 154.7 %reduce-scatter.4.cloned.1.call-start = ((), (), s32[]{:S(2)}) async-start(), calls=%async_computation.6 | async-start | bytes 1114112 | tf_op jit(solution)/shard_map/reduce_scatter | solution.py:136
  67.5 5.7 %copy-start.5 = (f32[27,32,512]{2,1,0:T(8,128)S(1)}, f32[27,32,512]{2,1,0:T(8,128)}, u32[]{:S(2)}) copy-start(f32[27,32,512]{2,1,0:T(8,128)} %param.9) | copy-start | bytes 5308420
  73.2 5.4 %copy-start.2 = (f32[512,16,128]{2,0,1:T(8,128)S(1)}, f32[512,16,128]{2,0,1:T(8,128)}, u32[]{:S(2)}) copy-start(f32[512,16,128]{2,0,1:T(8,128)} %copy.118) | copy-start | bytes 12582916
  108.4 62.0 %copy-start.6 = (f32[8,64,512]{2,1,0:T(8,128)S(1)}, f32[8,64,512]{2,1,0:T(8,128)}, u32[]{:S(2)}) copy-start(f32[8,64,512]{2,1,0:T(8,128)} %param.12) | copy-start | bytes 3145732
  112.7 100.4 %all-gather.6.cloned.1.call-start = ((), (), s32[]{:S(2)}) async-start(), calls=%async_computation.2 | async-start | bytes 1114112 | tf_op jit(solution)/shard_map/all_gather | solution.py:144
  173.5 72.5 %all-to-all-start = ((f32[16,1,16384]{2,1,0:T(1,128)}), f32[16,1,16384]{2,1,0:T(1,128)S(1)}, u32[]{:S(2)}, u32[]{:S(2)}) async-start(f32[16,1,16384]{2,1,0:T(1,128)} %reshape.464), calls=%async_computation | async-start | bytes 2097152 | tf_op jit(solution)/shard_map/all_to_all | solution.py:147
  177.2 105.4 %all-gather.8.cloned.1.call-start = ((), (), s32[]{:S(2)}) async-start(), calls=%async_computation.3 | async-start | bytes 1114112 | tf_op jit(solution)/shard_map/all_gather | solution.py:146
  213.1 3.0 copy-start.3
  245.7 91.5 %all-gather.10.cloned.1.call-start = ((), (), s32[]{:S(2)}) async-start(), calls=%async_computation.4 | async-start | bytes 4456448 | tf_op jit(solution)/shard_map/all_gather | solution.py:152
  342.5 3.7 %copy-start.1 = (f32[256,2,512]{2,1,0:T(2,128)S(1)}, f32[256,2,512]{2,1,0:T(2,128)}, u32[]{:S(2)}) copy-start(f32[256,2,512]{2,1,0:T(2,128)} %param.7) | copy-start | bytes 3145732
Sparse Core Ops, SparseCore 0:
  14.4 53.0 all-gather.11
  112.8 56.0 reduce-scatter.3
  171.1 41.9 all-gather.5
  245.8 36.8 all-gather.7
  287.8 49.3 all-gather.9
where the time goes:
time: 358 us; the launch traced here: 353 us
  waiting for transfers between devices  222 us (62%)
  matrix products  73.8 us (21%)
  local copies, waits for them, and re-layouts  23.3 us (7%)
  other arithmetic  15.5 us (4%)
  between operations  14.3 us (4%)
  starting transfers between devices  4.31 us (1%)
    reduce_scatter x1, waiting for transfers between devices, shards(): lax.psum_scatter(jnp.einsum('tco,tcn->on', w_down_mid, deep_stack, precis...  56.2 us
    all_gather x1, waiting for transfers between devices, shards(): shard_piece = lax.all_gather(mid_input, 'wide', axis=1, tiled=True)  53 us
    all_gather x1, waiting for transfers between devices, shards(): merged_every = lax.all_gather(mid_merged, 'wide', axis=0, tiled=True)  49.5 us
    all_gather x1, waiting for transfers between devices, shards(): lax.all_gather(deep_part, 'wide', axis=0, tiled=True)  35.6 us
    dot_general x9, matrix products, shards(): jnp.einsum('aoc,ckn->aokn', mid_kernel[:, convolve_b, convolve_c], shifte...  30.2 us
    all_gather x1, waiting for transfers between devices, shards(): deep_every = lax.all_gather(deep_output, 'wide', axis=0, tiled=True)  27.6 us
    dot_general x3, matrix products, convolve_deep(): jnp.einsum('tok,tkn->on', deep_kernel[a].reshape(9, deep_local, row_count...  22.7 us
    unnamed x8, other arithmetic  8.85 us
  transfers between devices with their start and end apart: 6, of which 5 were waited for; matrix products, arithmetic and copies ran while one was open for 12% of the time, Pallas kernels for 0%

commit v1 on v0

v1 whole, which is shorter than its diff:
```python
import functools

import jax
import jax.numpy as jnp
from jax import lax
from jax.experimental import pallas as pl
from jax.experimental.pallas import tpu as pltpu
from jax.sharding import PartitionSpec as P

YA = 32
ZA = 16
MID_ROWS, MID_COLS = YA // 2, ZA // 2
MID_CELLS = MID_ROWS * MID_COLS
DEEP_ROWS, DEEP_COLS = YA // 4, ZA // 4
DEEP_CELLS = DEEP_ROWS * DEEP_COLS
LANES = 128
PACK = LANES // DEEP_CELLS
SMEM = pl.BlockSpec(memory_space=pltpu.SMEM)
VMEM = pl.BlockSpec(memory_space=pltpu.VMEM)


def split_outside(weights):
    rounded = lax.reduce_precision(weights, 8, 7)
    return rounded.astype(jnp.bfloat16), (weights - rounded).astype(jnp.bfloat16)


def split_inside(values):
    high = values.astype(jnp.bfloat16)
    return high, (values - high.astype(jnp.float32)).astype(jnp.bfloat16)


def product(left, right):
    return jnp.dot(left, right, preferred_element_type=jnp.float32)


def product_three(left_high, left_low, right_high, right_low):
    return (
        product(left_high, right_high)
        + product(left_high, right_low)
        + product(left_low, right_high)
    )


def picker(blocks, rows, cols):
    small_rows, small_cols = rows // 2, cols // 2
    big = jnp.arange(blocks * rows * cols)[:, None]
    small = jnp.arange(4 * blocks * small_rows * small_cols)[None, :]
    cells = small_rows * small_cols
    tap, block, cell = small // (blocks * cells), small // cells % blocks, small % cells
    row = 2 * (cell // small_cols) + tap // 2
    col = 2 * (cell % small_cols) + tap % 2
    return (big == (block * rows + row) * cols + col).astype(jnp.bfloat16)


def inside(places, limit, step):
    moved = places + step
    return (moved >= 0) & (moved < limit)


def down_fine_kernel(field_ref, place_ref, weight_ref, out_ref, total_ref):
    step = pl.program_id(0)

    def gather(a):
        high, low = split_inside(field_ref[:, a, :])
        return [
            lax.dot_general(place_ref[...], part, (((1,), (1,)), ((), ())), preferred_element_type=jnp.float32).astype(
                jnp.bfloat16
            )
            for part in (high, low)
        ]

    for a in range(2):

        @pl.when(step == a)
        def _():
            high, low = gather(a)
            total = jnp.zeros(total_ref.shape, jnp.float32) if a == 0 else total_ref[...]
            for tap in range(4):
                weight_high, weight_low = split_inside(weight_ref[tap])
                block = slice(tap * MID_CELLS, (tap + 1) * MID_CELLS)
                total = total + product_three(high[block], low[block], weight_high, weight_low)
            if a == 0:
                total_ref[...] = total
            else:
                out_ref[...] = total.T


def down_fine(field, place, weights):
    chan_fine, chan_mid = weights.shape[1:]
    return pl.pallas_call(
        down_fine_kernel,
        out_shape=jax.ShapeDtypeStruct((chan_mid, MID_CELLS), jnp.float32),
        grid=(2,),
        in_specs=[
            pl.BlockSpec(field.shape, lambda a: (0, 0, 0)),
            pl.BlockSpec(place.shape, lambda a: (0, 0)),
            pl.BlockSpec((4, chan_fine, chan_mid), lambda a: (a, 0, 0)),
        ],
        out_specs=pl.BlockSpec((chan_mid, MID_CELLS), lambda a: (0, 0)),
        scratch_shapes=[pltpu.VMEM((MID_CELLS, chan_mid), jnp.float32)],
        name="down_fine",
    )(field, place, weights)


def plane_at(me, step, other, chips):
    chip, core = me // 2, me % 2
    position = jnp.where(chip % 2 == 0, chip // 2, chips - 1 - chip // 2)
    position = (position + step + chips) % chips
    chip = jnp.where(position < chips // 2, 2 * position, 2 * (chips - 1 - position) + 1)
    return 2 * chip + (1 - core if other else core)


def conv_mid_add(me, chips, places, high_ref, low_ref, fields, sum_ref):
    rows = sum_ref.shape[1]
    field_high, field_low = split_inside(jnp.concatenate(fields, axis=1))
    place = lax.broadcasted_iota(jnp.int32, (rows, LANES), 1)
    row_of, col_of = place // MID_COLS, place % MID_COLS
    for a in range(3):
        block = pl.ds(a * 9 * rows, 9 * rows)
        spread = product_three(high_ref[block, :], low_ref[block, :], field_high, field_low)
        for side, (step, other) in enumerate(places):
            total = jnp.zeros((rows, LANES), jnp.float32)
            for b in range(3):
                for c in range(3):
                    tap = 3 * b + c
                    piece = spread[tap * rows : (tap + 1) * rows, side * LANES : (side + 1) * LANES]
                    offset = (b - 1) * MID_COLS + (c - 1)
                    if offset:
                        piece = pltpu.roll(piece, (-offset) % LANES, 1)
                        keep = inside(row_of, MID_ROWS, b - 1) & inside(col_of, MID_COLS, c - 1)
                        piece = jnp.where(keep, piece, 0.0)
                    total = total + piece
            plane = plane_at(me, step, other, chips) + (2 - a)
            sum_ref[plane] = sum_ref[plane] + total


def join(pieces):
    return pieces[0][...] if len(pieces) == 1 else jnp.concatenate([piece[...] for piece in pieces], axis=0)


def conv_mid_kernel(chips, places, parts, first, me_ref, high_ref, low_ref, *refs):
    sum_ref = refs[-1]
    if first:
        sum_ref[...] = jnp.zeros_like(sum_ref)
    else:
        sum_ref[...] = refs[-2][...]
    fields, at = [], 0
    for count in parts:
        fields.append(join(refs[at : at + count]))
        at += count
    conv_mid_add(me_ref[0], chips, places, high_ref, low_ref, fields, sum_ref)


def conv_mid(me, high, low, given, running, planes):
    rows = high.shape[0] // 27
    places = [(step, other) for _, step, other in given]
    fields = [piece for pieces, _, _ in given for piece in pieces]
    parts = [len(pieces) for pieces, _, _ in given]
    arrays = [me, high, low] + fields + ([] if running is None else [running])
    return pl.pallas_call(
        functools.partial(conv_mid_kernel, planes // 2, places, parts, running is None),
        out_shape=jax.ShapeDtypeStruct((planes + 2, rows, LANES), jnp.float32),
        in_specs=[SMEM] + [VMEM] * (len(arrays) - 1),
        out_specs=VMEM,
        input_output_aliases={} if running is None else {len(arrays) - 1: 0},
        name="conv_mid",
    )(*arrays)


def down_mid_kernel(chips, places, parts, me_ref, high_ref, low_ref, pick_ref, weight_ref, *refs):
    running_ref, mid_ref, part_ref, sum_ref = refs[-4:]
    sum_ref[...] = running_ref[...]
    fields, at = [], 0
    for count in parts:
        fields.append(join(refs[at : at + count]))
        at += count
    conv_mid_add(me_ref[0], chips, places, high_ref, low_ref, fields, sum_ref)
    planes = mid_ref.shape[0]
    groups = planes // 2 // PACK
    mid_ref[...] = jnp.maximum(sum_ref[1 : planes + 1], 0.0)
    rows = mid_ref.shape[1]
    lines = []
    for a in range(2):
        for g in range(groups):
            lines.append(jnp.concatenate([mid_ref[2 * (g * PACK + q) + a] for q in range(PACK)], axis=1))
    high, low = split_inside(jnp.concatenate(lines, axis=0))
    picks = []
    for part in (high, low):
        moved = product(part, pick_ref[...]).astype(jnp.bfloat16)
        taps = []
        for a in range(2):
            for tap in range(4):
                taps.append(
                    jnp.concatenate(
                        [
                            moved[(a * groups + g) * rows : (a * groups + g + 1) * rows, tap * LANES : (tap + 1) * LANES]
                            for g in range(groups)
                        ],
                        axis=1,
                    )
                )
        picks.append(jnp.concatenate(taps, axis=0))
    weight_high, weight_low = split_inside(weight_ref[...])
    part_ref[...] = product_three(weight_high, weight_low, picks[0], picks[1])


def down_mid(me, high, low, pick, weight, given, running, planes):
    rows = high.shape[0] // 27
    places = [(step, other) for _, step, other in given]
    fields = [piece for pieces, _, _ in given for piece in pieces]
    parts = [len(pieces) for pieces, _, _ in given]
    arrays = [me, high, low, pick, weight] + fields + [running]
    return pl.pallas_call(
        functools.partial(down_mid_kernel, planes // 2, places, parts),
        out_shape=(
            jax.ShapeDtypeStruct((planes, rows, LANES), jnp.float32),
            jax.ShapeDtypeStruct((weight.shape[0], planes // 2 * DEEP_CELLS), jnp.float32),
        ),
        in_specs=[SMEM] + [VMEM] * (len(arrays) - 1),
        out_specs=(VMEM, VMEM),
        scratch_shapes=[pltpu.VMEM(running.shape, jnp.float32)],
        name="down_mid",
    )(*arrays)


def reversed_bits(value, blocks):
    width = blocks.bit_length() - 1
    return sum(((value >> k) & 1) << (width - 1 - k) for k in range(width))


def sorted_split(me, field_ref, high_ref, low_ref, blocks, whole):
    size = field_ref.shape[0] // blocks
    for block in range(blocks):
        source = reversed_bits(block ^ me, blocks) if whole else block ^ reversed_bits(me % blocks, blocks)
        source = pl.multiple_of(source * size, size)
        high, low = split_inside(field_ref[pl.ds(source, size), :])
        high_ref[pl.ds(block * size, size), :] = high
        low_ref[pl.ds(block * size, size), :] = low


def conv_deep_kernel(blocks, me_ref, weight_ref, field_ref, out_ref, field_high, field_low):
    a = pl.program_id(0)
    rows, cells = out_ref.shape

    @pl.when(a == 0)
    def _():
        sorted_split(me_ref[0], field_ref, field_high, field_low, blocks, False)
        out_ref[...] = jnp.zeros_like(out_ref)

    weight_high, weight_low = split_inside(weight_ref[...])
    spread = product_three(weight_high, weight_low, field_high[...], field_low[...])
    place = lax.broadcasted_iota(jnp.int32, (rows, cells), 1)
    plane_of = place // DEEP_CELLS
    row_of, col_of = place // DEEP_COLS % DEEP_ROWS, place % DEEP_COLS
    total = jnp.zeros((rows, cells), jnp.float32)
    for b in range(3):
        for c in range(3):
            tap = 3 * b + c
            piece = spread[tap * rows : (tap + 1) * rows]
            offset = (b - 1) * DEEP_COLS + (c - 1)
            if offset:
                piece = pltpu.roll(piece, (-offset) % cells, 1)
                keep = inside(row_of, DEEP_ROWS, b - 1) & inside(col_of, DEEP_COLS, c - 1)
                piece = jnp.where(keep, piece, 0.0)
            total = total + piece
    for step in range(3):

        @pl.when(a == step)
        def _():
            moved = total
            if step != 1:
                moved = pltpu.roll(moved, (-(step - 1) * DEEP_CELLS) % cells, 1)
                moved = jnp.where(inside(plane_of, cells // DEEP_CELLS, step - 1), moved, 0.0)
            summed = out_ref[...] + moved
            out_ref[...] = jnp.maximum(summed, 0.0) if step == 2 else summed


def conv_deep(me, blocks, weight, field):
    rows = weight.shape[0] // 27
    depth, cells = field.shape
    return pl.pallas_call(
        functools.partial(conv_deep_kernel, blocks),
        out_shape=jax.ShapeDtypeStruct((rows, cells), jnp.float32),
        grid=(3,),
        in_specs=[
            SMEM,
            pl.BlockSpec((9 * rows, depth), lambda a: (a, 0)),
            pl.BlockSpec((depth, cells), lambda a: (0, 0)),
        ],
        out_specs=pl.BlockSpec((rows, cells), lambda a: (0, 0)),
        scratch_shapes=[pltpu.VMEM((depth, cells), jnp.bfloat16)] * 2,
        name="conv_deep",
    )(me, weight, field)


def up_deep_kernel(blocks, me_ref, weight_ref, field_ref, place_ref, mid_ref, out_ref, field_high, field_low):
    sorted_split(me_ref[0], field_ref, field_high, field_low, blocks, True)
    planes, rows, _ = mid_ref.shape
    groups = planes // 2 // PACK
    size = weight_ref.shape[2] // 8
    weight = jnp.concatenate(
        [
            jnp.concatenate([weight_ref[block, :, tap * size : (tap + 1) * size] for block in range(blocks)], axis=1)
            for tap in range(8)
        ],
        axis=0,
    )
    weight_high, weight_low = split_inside(weight)
    spread = product_three(weight_high, weight_low, field_high[...], field_low[...])
    lines = []
    for a in range(2):
        for g in range(groups):
            lines.append(
                jnp.concatenate(
                    [
                        spread[(4 * a + tap) * rows : (4 * a + tap + 1) * rows, g * LANES : (g + 1) * LANES]
                        for tap in range(4)
                    ],
                    axis=1,
                )
            )
    high, low = split_inside(jnp.concatenate(lines, axis=0))
    lifted = product(high, place_ref[...]) + product(low, place_ref[...])
    for a in range(2):
        for g in range(groups):
            for q in range(PACK):
                plane = 2 * (g * PACK + q) + a
                line = (a * groups + g) * rows
                piece = lifted[line : line + rows, q * LANES : (q + 1) * LANES]
                out_ref[plane] = jnp.maximum(mid_ref[plane] + piece, 0.0)


def up_deep(me, blocks, weight, field, place, mid):
    return pl.pallas_call(
        functools.partial(up_deep_kernel, blocks),
        out_shape=jax.ShapeDtypeStruct(mid.shape, jnp.float32),
        in_specs=[SMEM] + [VMEM] * 4,
        out_specs=VMEM,
        scratch_shapes=[pltpu.VMEM(field.shape, jnp.bfloat16)] * 2,
        name="up_deep",
    )(me, weight, field, place, mid)


def up_mid_kernel(weight_ref, field_ref, place_ref, out_ref, field_high, field_low):
    step = pl.program_id(0)

    @pl.when(step == 0)
    def _():
        field = field_ref[...].reshape(-1, LANES).T
        field_high[...], field_low[...] = split_inside(field)

    lines = []
    for tap in range(4):
        weight_high, weight_low = split_inside(weight_ref[tap])
        lines.append(product_three(field_high[...], field_low[...], weight_high, weight_low))
    high, low = split_inside(jnp.concatenate(lines, axis=0).T)
    lifted = product(high, place_ref[...]) + product(low, place_ref[...])
    for a in range(2):

        @pl.when(step == a)
        def _():
            out_ref[:, a, :] = lifted


def up_mid(weights, field, place):
    chan_mid, chan_fine = weights.shape[1:]
    return pl.pallas_call(
        up_mid_kernel,
        out_shape=jax.ShapeDtypeStruct((chan_fine, 2, place.shape[1]), jnp.float32),
        grid=(2,),
        in_specs=[
            pl.BlockSpec((4, chan_mid, chan_fine), lambda a: (a, 0, 0)),
            pl.BlockSpec(field.shape, lambda a: (0, 0, 0)),
            pl.BlockSpec(place.shape, lambda a: (0, 0)),
        ],
        out_specs=pl.BlockSpec((chan_fine, 2, place.shape[1]), lambda a: (0, 0, 0)),
        scratch_shapes=[pltpu.VMEM((MID_CELLS, chan_mid), jnp.bfloat16)] * 2,
        name="up_mid",
    )(weights, field, place)


def swap(field, bit):
    count = lax.axis_size("wide")
    return lax.ppermute(field, "wide", [(i, i ^ bit) for i in range(count)])


def shards(fine_field, w_down_fine, w_conv_mid, w_down_mid, w_conv_deep, w_up_deep, w_up_mid):
    count = lax.axis_size("wide")
    me = lax.axis_index("wide")
    me_array = me.astype(jnp.int32).reshape(1)
    chips = count // 2
    bits = [1 << k for k in range(count.bit_length() - 1)]
    mid_local, chan_mid = w_conv_mid.shape[1:]
    deep_local, chan_deep = w_conv_deep.shape[1:]
    pick_fine = picker(1, YA, ZA)
    pick_mid = picker(PACK, MID_ROWS, MID_COLS)

    mid_input = down_fine(fine_field, pick_fine.T, w_down_fine)

    conv_high, conv_low = split_outside(w_conv_mid.reshape(27 * mid_local, chan_mid))
    down_weight = w_down_mid.reshape(8 * mid_local, chan_deep).T
    w_rows = w_up_deep.reshape(8 * deep_local, chan_mid).T.reshape(count, mid_local, 8 * deep_local)

    ring = list(range(0, chips, 2)) + list(range(chips - 1, 0, -2))
    ahead = [
        (2 * ring[k] + core, 2 * ring[(k + 1) % chips] + core) for core in range(2) for k in range(chips)
    ]
    behind = [(target, source) for source, target in ahead]

    half = chan_mid // 2
    steps = chips // 2
    front = back = mid_input
    running = None
    queue = [((mid_input,), 0, False), ((swap(mid_input, 1),), 0, True)]
    for step in range(1, steps):
        front = lax.ppermute(front, "wide", ahead)
        back = lax.ppermute(back, "wide", behind)
        if step > 1:
            given, queue = queue, []
            running = conv_mid(me_array, conv_high, conv_low, given, running, count)
            front, back, running = lax.optimization_barrier((front, back, running))
        queue += [((front,), -step, False), ((back,), step, False)]
        held = [((swap(front, 1),), -step, True), ((swap(back, 1),), step, True)]
        if step == 1:
            later = held
        else:
            queue = later + queue
            later = held
    upper = lax.ppermute(front[:half], "wide", ahead)
    lower = lax.ppermute(back[half:], "wide", behind)
    running = conv_mid(me_array, conv_high, conv_low, queue, running, count)
    given = later + [((upper, lower), steps, False), ((swap(upper, 1), swap(lower, 1)), steps, True)]
    mid_field, part = down_mid(me_array, conv_high, conv_low, pick_mid, down_weight, given, running, count)

    held = part
    for bit in bits[:-1]:
        size = held.shape[0] // 2
        mine = (me // bit) % 2
        keep = lax.dynamic_slice_in_dim(held, mine * size, size, 0)
        send = lax.dynamic_slice_in_dim(held, (1 - mine) * size, size, 0)
        held = keep + swap(send, bit)
    held = jax.nn.relu(held + swap(held, bits[-1]))
    for bit in bits[-2::-1]:
        held = jnp.concatenate([held, swap(held, bit)], axis=0)
    deep_output = conv_deep(me_array, count // 2, w_conv_deep.reshape(27 * deep_local, chan_deep), held)

    w_columns = lax.all_to_all(w_rows, "wide", split_axis=0, concat_axis=0, tiled=True)
    held = deep_output
    for bit in bits[::-1]:
        held = jnp.concatenate([held, swap(held, bit)], axis=0)
    merged = up_deep(me_array, count, w_columns, held, pick_mid.T, mid_field)

    plane = lax.all_to_all(merged, "wide", split_axis=0, concat_axis=0, tiled=True)
    return up_mid(w_up_mid, plane, pick_fine.T)


def solution(mesh):
    return jax.shard_map(
        shards,
        mesh=mesh,
        in_specs=(
            P(None, ("groups", "wide"), None),
            P(),
            P(None, "wide", None),
            P(None, "wide", None),
            P(None, "wide", None),
            P(None, "wide", None),
            P(),
        ),
        out_specs=P(None, ("groups", "wide"), None),
        check_vma=False,
    )
```

time: 358 us -> 170 us (0.47); the launches traced: 353 us -> 169 us
  waiting for transfers between devices: 222 us -> 70.5 us
  matrix products: 73.8 us -> 0 us
  Pallas kernels: 0 us -> 41.6 us
  starting transfers between devices: 4.31 us -> 25.9 us
  local copies, waits for them, and re-layouts: 23.3 us -> 8.07 us
  blocking collectives: 0 us -> 14.2 us
  between operations: 14.3 us -> 0.37 us
  other arithmetic: 15.5 us -> 8.41 us
    all_gather x4 -> x0, waiting for transfers between devices: 166 us -> none  [the longest x1 53 us: shards(): shard_piece = lax.all_gather(mid_input, 'wide', axis=1, tiled=True)]
    dot_general x31 -> x0, matrix products: 71.5 us -> none  [the longest x9 30.2 us: shards(): jnp.einsum('aoc,ckn->aokn', mid_kernel[:, convolve_b, convolve_c], shifte...]
    ppermute x0 -> x28, waiting for transfers between devices: none -> 70.5 us  [the longest x20 58.7 us: swap(): return lax.ppermute(field, 'wide', [(i, i ^ bit) for i in range(count)])]
    reduce_scatter x1 -> x0, waiting for transfers between devices: 56.2 us -> none  [shards(): lax.psum_scatter(jnp.einsum('tco,tcn->on', w_down_mid, deep_stack, precis...]
    pallas_call x0 -> x8, Pallas kernels: none -> 41.6 us  [the longest x3 12.6 us: conv_mid(): pl.pallas_call(functools.partial(conv_mid_kernel, planes // 2, places, pa...]
    ppermute x0 -> x28, starting transfers between devices: none -> 21.7 us  [the longest x20 12.3 us: swap(): return lax.ppermute(field, 'wide', [(i, i ^ bit) for i in range(count)])]
    all_to_all x0 -> x1, blocking collectives: none -> 14.2 us  [shards(): lax.all_to_all(merged, 'wide', split_axis=0, concat_axis=0, tiled=True)]
    unnamed x8 -> x0, other arithmetic: 8.85 us -> none
  transfers between devices with their start and end apart: 6 -> 29, of which waited for: 5 -> 15; matrix products, arithmetic and copies ran while one was open for 12% -> 5% of each run, Pallas kernels for 0% -> 11%
where the time goes in v1:
time: 170 us; the launch traced here: 169 us
  waiting for transfers between devices  70.5 us (41%)
  Pallas kernels  41.6 us (24%)
  starting transfers between devices  25.9 us (15%)
  blocking collectives  14.2 us (8%)
  other arithmetic  8.41 us (5%)
  local copies, waits for them, and re-layouts  8.07 us (5%)
    ppermute x20, waiting for transfers between devices, swap(): return lax.ppermute(field, 'wide', [(i, i ^ bit) for i in range(count)])  58.7 us
    all_to_all x1, blocking collectives, shards(): lax.all_to_all(merged, 'wide', split_axis=0, concat_axis=0, tiled=True)  14.2 us
    pallas_call x3, Pallas kernels, conv_mid(): pl.pallas_call(functools.partial(conv_mid_kernel, planes // 2, places, pa...  12.6 us
    ppermute x20, starting transfers between devices, swap(): return lax.ppermute(field, 'wide', [(i, i ^ bit) for i in range(count)])  12.3 us
    ppermute x3, waiting for transfers between devices, shards(): front = lax.ppermute(front, 'wide', ahead)  7.71 us
    pallas_call x1, Pallas kernels, down_fine(): pl.pallas_call(down_fine_kernel, out_shape=jax.ShapeDtypeStruct((chan_mid...  7.6 us
    pallas_call x1, Pallas kernels, conv_deep(): pl.pallas_call(functools.partial(conv_deep_kernel, blocks), out_shape=jax...  6.83 us
    ppermute x3, starting transfers between devices, shards(): front = lax.ppermute(front, 'wide', ahead)  6.7 us
  transfers between devices with their start and end apart: 29, of which 15 were waited for; matrix products, arithmetic and copies ran while one was open for 5% of the time, Pallas kernels for 11%

profile of v1, /device:TPU:0, one launch (start us, length us, event | category | flops | bytes accessed | tf_op | source)
XLA Modules:
  0.0 169.1 jit_solution(10317309065560656539)
XLA Ops:
  1.0 7.6 %down_fine.1.refs_0_ = f32[512,128]{1,0:T(8,128)} custom-call(f32[256,2,512]{2,1,0:T(2,128)} %field_ref.1, bf16[512,512]{1,0:T(8,128)(2,1)} %fusion.2.place_ref, f32[8,256,512]{2,1,0:T(8,128)} %weight_ref.2), custom_call_target="tpu_custom_call" | custom-call | tf_op jit(solution)/shard_map/down_fine/pallas_call | solution.py:90
  8.6 3.1 %collective-permute-start = (f32[512,128]{1,0:T(8,128)}, f32[512,128]{1,0:T(8,128)S(1)}, u32[]{:S(2)}, u32[]{:S(2)}) collective-permute-start(f32[512,128]{1,0:T(8,128)} %down_fine.1.refs_0_), channel_id=1, source_target_pairs={{0,4},{4,8},{8,12},{12,14},{14,10},{10,6},{6,2},{2,0},{1,5},{5,9},... | collective-permute-start | bytes 786440 | tf_op jit(solution)/shard_map/ppermute | solution.py:416
  11.6 6.4 %collective-permute-done.refs_2_ = f32[512,128]{1,0:T(8,128)S(1)} collective-permute-done((f32[512,128]{1,0:T(8,128)}, f32[512,128]{1,0:T(8,128)S(1)}, u32[]{:S(2)}, u32[]{:S(2)}) %collective-permute-start) | collective-permute-done | bytes 262176 | tf_op jit(solution)/shard_map/ppermute | solution.py:416
  22.8 4.2 %conv_mid.3.refs_4_ = f32[18,32,128]{2,1,0:T(8,128)} custom-call(s32[1]{0:T(128)} %bitcast.me_ref, bf16[864,512]{1,0:T(8,128)(2,1)} %get-tuple-element.22.high_ref, bf16[864,512]{1,0:T(8,128)(2,1)} %get-tuple-element.21.low_ref, f32[512,128]{1,0:T(8,128)} %down_fine.1.refs_0_, f32[512,128]{1,0:T(8,128)} %copy-done.17, f32[512,128]{1,0:T(8,128)} %copy-done.14, ...), custom_call_target="tpu_custom_call" | custom-call | tf_op jit(solution)/shard_map/conv_mid/pallas_call | solution.py:160
  27.0 1.9 %collective-permute-start.5 = (f32[512,128]{1,0:T(8,128)S(1)}, f32[512,128]{1,0:T(8,128)S(1)}, u32[]{:S(2)}, u32[]{:S(2)}) collective-permute-start(f32[512,128]{1,0:T(8,128)S(1)} %collective-permute-done.1.refs_2_), channel_id=1, source_target_pairs={{0,4},{4,8},{8,12},{12,14},{14,10},{10,6},{6,2},{2,0},{1,5},{5,9},... | collective-permute-start | bytes 786440 | tf_op jit(solution)/shard_map/ppermute | solution.py:416
  29.7 4.2 %conv_mid.4.refs_4_ = f32[18,32,128]{2,1,0:T(8,128)} custom-call(s32[1]{0:T(128)} %bitcast.me_ref, bf16[864,512]{1,0:T(8,128)(2,1)} %get-tuple-element.22.high_ref, bf16[864,512]{1,0:T(8,128)(2,1)} %get-tuple-element.21.low_ref, f32[512,128]{1,0:T(8,128)} %copy-done.16, f32[512,128]{1,0:T(8,128)} %collective-permute-done.8.refs_1_, ...), custom_call_target="tpu_custom_call", output_to_operand_aliasing={{}: (7, {})} | custom-call | tf_op jit(solution)/shard_map/conv_mid/pallas_call | solution.py:160
  41.8 1.8 %collective-permute-done.12.refs_3_ = f32[256,128]{1,0:T(8,128)S(1)} collective-permute-done((f32[256,128]{1,0:T(8,128)S(1)}, f32[256,128]{1,0:T(8,128)S(1)}, u32[]{:S(2)}, u32[]{:S(2)}) %collective-permute-start.12) | collective-permute-done | bytes 131104 | tf_op jit(solution)/shard_map/ppermute | solution.py:430
  45.5 4.2 %conv_mid.5.refs_6_ = f32[18,32,128]{2,1,0:T(8,128)} custom-call(s32[1]{0:T(128)} %bitcast.me_ref, bf16[864,512]{1,0:T(8,128)(2,1)} %get-tuple-element.22.high_ref, bf16[864,512]{1,0:T(8,128)(2,1)} %get-tuple-element.21.low_ref, f32[512,128]{1,0:T(8,128)} %copy-done.9, f32[512,128]{1,0:T(8,128)} %copy-done.13, ...), custom_call_target="tpu_custom_call", output_to_operand_aliasing={{}: (7, {})} | custom-call | tf_op jit(solution)/shard_map/conv_mid/pallas_call | solution.py:160
  50.6 5.8 %down_mid.1 = (f32[16,32,128]{2,1,0:T(8,128)}, f32[1024,256]{1,0:T(8,128)}) custom-call(s32[1]{0:T(128)} %bitcast.me_ref, bf16[864,512]{1,0:T(8,128)(2,1)} %get-tuple-element.22.high_ref, bf16[864,512]{1,0:T(8,128)(2,1)} %get-tuple-element.21.low_ref, bf16[512,512]{1,0:T(8,128)(2,1)} %get-tuple-element.24.pick_ref, f32[1024,256]{1,0:T(8,128)} %bitcast.12, ...), custom_call_target="tpu_custom_call" | custom-call | tf_op jit(solution)/shard_map/down_mid/pallas_call | solution.py:213
  61.3 8.1 %collective-permute-done.18 = f32[256,256]{1,0:T(8,128)S(1)} collective-permute-done((f32[256,256]{1,0:T(8,128)S(1)}, f32[256,256]{1,0:T(8,128)S(1)}, u32[]{:S(2)}, u32[]{:S(2)}) %collective-permute-start.18) | collective-permute-done | bytes 262176 | tf_op jit(solution)/shard_map/ppermute | solution.py:384
  71.1 3.4 %collective-permute-done.19 = f32[128,256]{1,0:T(8,128)S(1)} collective-permute-done((f32[128,256]{1,0:T(8,128)S(1)}, f32[128,256]{1,0:T(8,128)S(1)}, u32[]{:S(2)}, u32[]{:S(2)}) %collective-permute-start.19) | collective-permute-done | bytes 131104 | tf_op jit(solution)/shard_map/ppermute | solution.py:384
  74.5 2.6 %collective-permute-start.20 = (f32[128,256]{1,0:T(8,128)S(1)}, f32[128,256]{1,0:T(8,128)S(1)}, u32[]{:S(2)}, u32[]{:S(2)}) collective-permute-start(f32[128,256]{1,0:T(8,128)S(1)} %dynamic-slice_add_fusion.2), channel_id=1, source_target_pairs={{0,8},{1,9},{2,10},{3,11},{4,12},{5,13},{6,14},{7,15},{8,0},{9,1},... | collective-permute-start | bytes 393224 | tf_op jit(solution)/shard_map/ppermute | solution.py:384
  77.1 4.9 %collective-permute-done.20 = f32[128,256]{1,0:T(8,128)S(1)} collective-permute-done((f32[128,256]{1,0:T(8,128)S(1)}, f32[128,256]{1,0:T(8,128)S(1)}, u32[]{:S(2)}, u32[]{:S(2)}) %collective-permute-start.20) | collective-permute-done | bytes 131104 | tf_op jit(solution)/shard_map/ppermute | solution.py:384
  82.2 4.9 %collective-permute-done.21 = f32[128,256]{1,0:T(8,128)S(1)} collective-permute-done((f32[128,256]{1,0:T(8,128)S(1)}, f32[128,256]{1,0:T(8,128)S(1)}, u32[]{:S(2)}, u32[]{:S(2)}) %collective-permute-start.21) | collective-permute-done | bytes 131104 | tf_op jit(solution)/shard_map/ppermute | solution.py:384
  88.2 5.4 %collective-permute-done.22 = f32[256,256]{1,0:T(8,128)S(1)} collective-permute-done((f32[256,256]{1,0:T(8,128)S(1)}, f32[256,256]{1,0:T(8,128)S(1)}, u32[]{:S(2)}, u32[]{:S(2)}) %collective-permute-start.22) | collective-permute-done | bytes 262176 | tf_op jit(solution)/shard_map/ppermute | solution.py:384
  95.0 4.2 %all-to-all-start = ((f32[16,32,512]{2,1,0:T(8,128)}), f32[16,32,512]{2,1,0:T(8,128)S(1)}, u32[]{:S(2)}, u32[]{:S(2)}) async-start(f32[16,32,512]{2,1,0:T(8,128)} %bitcast.3), calls=%async_computation | async-start | bytes 2097152 | tf_op jit(solution)/shard_map/all_to_all | solution.py:447
  100.2 6.8 %conv_deep.1 = f32[64,256]{1,0:T(8,128)} custom-call(s32[1]{0:T(128)} %bitcast.me_ref, f32[1728,1024]{1,0:T(8,128)} %bitcast.11, f32[1024,256]{1,0:T(8,128)} %pad_maximum_fusion.field_ref), custom_call_target="tpu_custom_call" | custom-call | tf_op jit(solution)/shard_map/conv_deep/pallas_call | solution.py:281
  107.1 2.8 %collective-permute-start.24 = (f32[64,256]{1,0:T(8,128)}, f32[64,256]{1,0:T(8,128)S(1)}, u32[]{:S(2)}, u32[]{:S(2)}) collective-permute-start(f32[64,256]{1,0:T(8,128)} %conv_deep.1), channel_id=1, source_target_pairs={{0,8},{1,9},{2,10},{3,11},{4,12},{5,13},{6,14},{7,15},{8,0},{9,1},... | collective-permute-start | bytes 196616 | tf_op jit(solution)/shard_map/ppermute | solution.py:384
  109.9 18.6 %collective-permute-done.24 = f32[64,256]{1,0:T(8,128)S(1)} collective-permute-done((f32[64,256]{1,0:T(8,128)}, f32[64,256]{1,0:T(8,128)S(1)}, u32[]{:S(2)}, u32[]{:S(2)}) %collective-permute-start.24) | collective-permute-done | bytes 65568 | tf_op jit(solution)/shard_map/ppermute | solution.py:384
  129.4 5.0 %collective-permute-done.25 = f32[128,256]{1,0:T(8,128)S(1)} collective-permute-done((f32[128,256]{1,0:T(8,128)S(1)}, f32[128,256]{1,0:T(8,128)S(1)}, u32[]{:S(2)}, u32[]{:S(2)}) %collective-permute-start.25) | collective-permute-done | bytes 131104 | tf_op jit(solution)/shard_map/ppermute | solution.py:384
  136.8 5.1 %collective-permute-done.26 = f32[256,256]{1,0:T(8,128)S(1)} collective-permute-done((f32[256,256]{1,0:T(8,128)S(1)}, f32[256,256]{1,0:T(8,128)S(1)}, u32[]{:S(2)}, u32[]{:S(2)}) %collective-permute-start.26) | collective-permute-done | bytes 262176 | tf_op jit(solution)/shard_map/ppermute | solution.py:384
  146.1 3.6 %up_deep.1 = f32[16,32,128]{2,1,0:T(8,128)} custom-call(s32[1]{0:T(128)} %bitcast.me_ref, f32[16,32,512]{2,1,0:T(8,128)} %copy-done, f32[1024,256]{1,0:T(8,128)} %copy-done.3, bf16[512,512]{1,0:T(8,128)(2,1)} %get-tuple-element.23.place_ref, f32[16,32,128]{2,1,0:T(8,128)} %get-tuple-element.20.mid_ref), custom_call_target="tpu_custom_call" | custom-call | tf_op jit(solution)/shard_map/up_deep/pallas_call | solution.py:334
  149.7 14.2 %all_to_all.10.field_ref = f32[16,32,128]{2,1,0:T(8,128)} all-to-all(f32[16,32,128]{2,1,0:T(8,128)} %up_deep.1), channel_id=1, replica_groups=mesh['groups'=2,'wide'=16] {'wide'}, dimensions={0} | all-to-all | bytes 524288 | tf_op jit(solution)/shard_map/all_to_all | solution.py:453
  163.9 5.2 %up_mid.1 = f32[256,2,512]{2,1,0:T(2,128)} custom-call(f32[8,512,256]{2,1,0:T(8,128)} %weight_ref.3, f32[16,32,128]{2,1,0:T(8,128)} %all_to_all.10.field_ref, bf16[512,512]{1,0:T(8,128)(2,1)} %fusion.2.place_ref), custom_call_target="tpu_custom_call" | custom-call | tf_op jit(solution)/shard_map/up_mid/pallas_call | solution.py:367
  (114 shorter events, 34.8 us)
Async XLA Ops:
  8.6 9.5 %collective-permute-start = (f32[512,128]{1,0:T(8,128)}, f32[512,128]{1,0:T(8,128)S(1)}, u32[]{:S(2)}, u32[]{:S(2)}) collective-permute-start(f32[512,128]{1,0:T(8,128)} %down_fine.1.refs_0_), channel_id=1, source_target_pairs={{0,4},{4,8},{8,12},{12,14},{14,10},{10,6},{6,2},{2,0},{1,5},{5,9},... | collective-permute-start | bytes 786440 | tf_op jit(solution)/shard_map/ppermute | solution.py:416
  11.6 8.3 %collective-permute-start.2 = (f32[512,128]{1,0:T(8,128)}, f32[512,128]{1,0:T(8,128)S(1)}, u32[]{:S(2)}, u32[]{:S(2)}) collective-permute-start(f32[512,128]{1,0:T(8,128)} %down_fine.1.refs_0_), channel_id=1, source_target_pairs={{4,0},{8,4},{12,8},{14,12},{10,14},{6,10},{2,6},{0,2},{5,1},{9,5},... | collective-permute-start | bytes 786440 | tf_op jit(solution)/shard_map/ppermute | solution.py:417
  11.6 10.4 %collective-permute-start.4 = (f32[512,128]{1,0:T(8,128)}, f32[512,128]{1,0:T(8,128)S(1)}, u32[]{:S(2)}, u32[]{:S(2)}) collective-permute-start(f32[512,128]{1,0:T(8,128)} %down_fine.1.refs_0_), channel_id=1, source_target_pairs={{0,1},{1,0},{2,3},{3,2},{4,5},{5,4},{6,7},{7,6},{8,9},{9,8},{10,11... | collective-permute-start | bytes 786440 | tf_op jit(solution)/shard_map/ppermute | solution.py:384
  18.1 8.8 %collective-permute-start.1 = (f32[512,128]{1,0:T(8,128)S(1)}, f32[512,128]{1,0:T(8,128)S(1)}, u32[]{:S(2)}, u32[]{:S(2)}) collective-permute-start(f32[512,128]{1,0:T(8,128)S(1)} %collective-permute-done.refs_2_), channel_id=1, source_target_pairs={{0,4},{4,8},{8,12},{12,14},{14,10},{10,6},{6,2},{2,0},{1,5},{5,9},... | collective-permute-start | bytes 786440 | tf_op jit(solution)/shard_map/ppermute | solution.py:416
  19.9 7.1 %collective-permute-start.3 = (f32[512,128]{1,0:T(8,128)S(1)}, f32[512,128]{1,0:T(8,128)S(1)}, u32[]{:S(2)}, u32[]{:S(2)}) collective-permute-start(f32[512,128]{1,0:T(8,128)S(1)} %collective-permute-done.2.refs_3_), channel_id=1, source_target_pairs={{4,0},{8,4},{12,8},{14,12},{10,14},{6,10},{2,6},{0,2},{5,1},{9,5},... | collective-permute-start | bytes 786440 | tf_op jit(solution)/shard_map/ppermute | solution.py:417
  21.6 7.5 %collective-permute-start.7 = (f32[512,128]{1,0:T(8,128)S(1)}, f32[512,128]{1,0:T(8,128)S(1)}, u32[]{:S(2)}, u32[]{:S(2)}) collective-permute-start(f32[512,128]{1,0:T(8,128)S(1)} %collective-permute-done.refs_2_), channel_id=1, source_target_pairs={{0,1},{1,0},{2,3},{3,2},{4,5},{5,4},{6,7},{7,6},{8,9},{9,8},{10,11... | collective-permute-start | bytes 786440 | tf_op jit(solution)/shard_map/ppermute | solution.py:384
  21.6 7.5 %collective-permute-start.8 = (f32[512,128]{1,0:T(8,128)S(1)}, f32[512,128]{1,0:T(8,128)}, u32[]{:S(2)}, u32[]{:S(2)}) collective-permute-start(f32[512,128]{1,0:T(8,128)S(1)} %collective-permute-done.2.refs_3_), channel_id=1, source_target_pairs={{0,1},{1,0},{2,3},{3,2},{4,5},{5,4},{6,7},{7,6},{8,9},{9,8},{10,11... | collective-permute-start | bytes 786440 | tf_op jit(solution)/shard_map/ppermute | solution.py:384
  27.0 8.3 %collective-permute-start.5 = (f32[512,128]{1,0:T(8,128)S(1)}, f32[512,128]{1,0:T(8,128)S(1)}, u32[]{:S(2)}, u32[]{:S(2)}) collective-permute-start(f32[512,128]{1,0:T(8,128)S(1)} %collective-permute-done.1.refs_2_), channel_id=1, source_target_pairs={{0,4},{4,8},{8,12},{12,14},{14,10},{10,6},{6,2},{2,0},{1,5},{5,9},... | collective-permute-start | bytes 786440 | tf_op jit(solution)/shard_map/ppermute | solution.py:416
  28.8 7.9 %collective-permute-start.6 = (f32[512,128]{1,0:T(8,128)S(1)}, f32[512,128]{1,0:T(8,128)S(1)}, u32[]{:S(2)}, u32[]{:S(2)}) collective-permute-start(f32[512,128]{1,0:T(8,128)S(1)} %collective-permute-done.3.refs_3_), channel_id=1, source_target_pairs={{4,0},{8,4},{12,8},{14,12},{10,14},{6,10},{2,6},{0,2},{5,1},{9,5},... | collective-permute-start | bytes 786440 | tf_op jit(solution)/shard_map/ppermute | solution.py:417
  29.0 10.6 %collective-permute-start.15 = (f32[512,128]{1,0:T(8,128)S(1)}, f32[512,128]{1,0:T(8,128)S(1)}, u32[]{:S(2)}, u32[]{:S(2)}) collective-permute-start(f32[512,128]{1,0:T(8,128)S(1)} %collective-permute-done.1.refs_2_), channel_id=1, source_target_pairs={{0,1},{1,0},{2,3},{3,2},{4,5},{5,4},{6,7},{7,6},{8,9},{9,8},{10,11... | collective-permute-start | bytes 786440 | tf_op jit(solution)/shard_map/ppermute | solution.py:384
  38.4 5.2 %collective-permute-start.12 = (f32[256,128]{1,0:T(8,128)S(1)}, f32[256,128]{1,0:T(8,128)S(1)}, u32[]{:S(2)}, u32[]{:S(2)}) collective-permute-start(f32[256,128]{1,0:T(8,128)S(1)} %slice.7), channel_id=1, source_target_pairs={{4,0},{8,4},{12,8},{14,12},{10,14},{6,10},{2,6},{0,2},{5,1},{9,5},... | collective-permute-start | bytes 393224 | tf_op jit(solution)/shard_map/ppermute | solution.py:430
  39.1 5.7 %collective-permute-start.16 = (f32[512,128]{1,0:T(8,128)}, f32[512,128]{1,0:T(8,128)S(1)}, u32[]{:S(2)}, u32[]{:S(2)}) collective-permute-start(f32[512,128]{1,0:T(8,128)} %copy-done.8), channel_id=1, source_target_pairs={{0,1},{1,0},{2,3},{3,2},{4,5},{5,4},{6,7},{7,6},{8,9},{9,8},{10,11... | collective-permute-start | bytes 786440 | tf_op jit(solution)/shard_map/ppermute | solution.py:384
  39.1 10.6 %collective-permute-start.10 = (f32[512,128]{1,0:T(8,128)S(1)}, f32[512,128]{1,0:T(8,128)S(1)}, u32[]{:S(2)}, u32[]{:S(2)}) collective-permute-start(f32[512,128]{1,0:T(8,128)S(1)} %collective-permute-done.6.refs_3_), channel_id=1, source_target_pairs={{0,1},{1,0},{2,3},{3,2},{4,5},{5,4},{6,7},{7,6},{8,9},{9,8},{10,11... | collective-permute-start | bytes 786440 | tf_op jit(solution)/shard_map/ppermute | solution.py:384
  39.6 10.2 %collective-permute-start.9 = (f32[512,128]{1,0:T(8,128)S(1)}, f32[512,128]{1,0:T(8,128)S(1)}, u32[]{:S(2)}, u32[]{:S(2)}) collective-permute-start(f32[512,128]{1,0:T(8,128)S(1)} %collective-permute-done.5.refs_2_), channel_id=1, source_target_pairs={{0,1},{1,0},{2,3},{3,2},{4,5},{5,4},{6,7},{7,6},{8,9},{9,8},{10,11... | collective-permute-start | bytes 786440 | tf_op jit(solution)/shard_map/ppermute | solution.py:384
  41.8 7.9 %collective-permute-start.13 = (f32[256,128]{1,0:T(8,128)S(1)}, f32[256,128]{1,0:T(8,128)S(1)}, u32[]{:S(2)}, u32[]{:S(2)}) collective-permute-start(f32[256,128]{1,0:T(8,128)S(1)} %collective-permute-done.11.refs_2_), channel_id=1, source_target_pairs={{0,1},{1,0},{2,3},{3,2},{4,5},{5,4},{6,7},{7,6},{8,9},{9,8},{10,11... | collective-permute-start | bytes 393224 | tf_op jit(solution)/shard_map/ppermute | solution.py:384
  43.6 6.1 %collective-permute-start.14 = (f32[256,128]{1,0:T(8,128)S(1)}, f32[256,128]{1,0:T(8,128)S(1)}, u32[]{:S(2)}, u32[]{:S(2)}) collective-permute-start(f32[256,128]{1,0:T(8,128)S(1)} %collective-permute-done.12.refs_3_), channel_id=1, source_target_pairs={{0,1},{1,0},{2,3},{3,2},{4,5},{5,4},{6,7},{7,6},{8,9},{9,8},{10,11... | collective-permute-start | bytes 393224 | tf_op jit(solution)/shard_map/ppermute | solution.py:384
  60.8 8.7 %collective-permute-start.18 = (f32[256,256]{1,0:T(8,128)S(1)}, f32[256,256]{1,0:T(8,128)S(1)}, u32[]{:S(2)}, u32[]{:S(2)}) collective-permute-start(f32[256,256]{1,0:T(8,128)S(1)} %constant_dynamic-slice_fusion.1), channel_id=1, source_target_pairs={{0,2},{1,3},{2,0},{3,1},{4,6},{5,7},{6,4},{7,5},{8,10},{9,11},{10,... | collective-permute-start | bytes 786440 | tf_op jit(solution)/shard_map/ppermute | solution.py:384
  69.5 5.0 %collective-permute-start.19 = (f32[128,256]{1,0:T(8,128)S(1)}, f32[128,256]{1,0:T(8,128)S(1)}, u32[]{:S(2)}, u32[]{:S(2)}) collective-permute-start(f32[128,256]{1,0:T(8,128)S(1)} %constant_dynamic-slice_fusion), channel_id=1, source_target_pairs={{0,4},{1,5},{2,6},{3,7},{4,0},{5,1},{6,2},{7,3},{8,12},{9,13},{10,... | collective-permute-start | bytes 393224 | tf_op jit(solution)/shard_map/ppermute | solution.py:384
  74.5 7.5 %collective-permute-start.20 = (f32[128,256]{1,0:T(8,128)S(1)}, f32[128,256]{1,0:T(8,128)S(1)}, u32[]{:S(2)}, u32[]{:S(2)}) collective-permute-start(f32[128,256]{1,0:T(8,128)S(1)} %dynamic-slice_add_fusion.2), channel_id=1, source_target_pairs={{0,8},{1,9},{2,10},{3,11},{4,12},{5,13},{6,14},{7,15},{8,0},{9,1},... | collective-permute-start | bytes 393224 | tf_op jit(solution)/shard_map/ppermute | solution.py:384
  87.1 6.4 %collective-permute-start.22 = (f32[256,256]{1,0:T(8,128)S(1)}, f32[256,256]{1,0:T(8,128)S(1)}, u32[]{:S(2)}, u32[]{:S(2)}) collective-permute-start(f32[256,256]{1,0:T(8,128)S(1)} %pad_maximum_fusion.3), channel_id=1, source_target_pairs={{0,2},{1,3},{2,0},{3,1},{4,6},{5,7},{6,4},{7,5},{8,10},{9,11},{10,... | collective-permute-start | bytes 786440 | tf_op jit(solution)/shard_map/ppermute | solution.py:384
  93.6 5.6 %collective-permute-start.23 = (f32[512,256]{1,0:T(8,128)S(1)}, f32[512,256]{1,0:T(8,128)S(1)}, u32[]{:S(2)}, u32[]{:S(2)}) collective-permute-start(f32[512,256]{1,0:T(8,128)S(1)} %pad_maximum_fusion.1), channel_id=1, source_target_pairs={{0,1},{1,0},{2,3},{3,2},{4,5},{5,4},{6,7},{7,6},{8,9},{9,8},{10,11... | collective-permute-start | bytes 1572872 | tf_op jit(solution)/shard_map/ppermute | solution.py:384
  95.0 49.8 %all-to-all-start = ((f32[16,32,512]{2,1,0:T(8,128)}), f32[16,32,512]{2,1,0:T(8,128)S(1)}, u32[]{:S(2)}, u32[]{:S(2)}) async-start(f32[16,32,512]{2,1,0:T(8,128)} %bitcast.3), calls=%async_computation | async-start | bytes 2097152 | tf_op jit(solution)/shard_map/all_to_all | solution.py:447
  107.1 21.4 %collective-permute-start.24 = (f32[64,256]{1,0:T(8,128)}, f32[64,256]{1,0:T(8,128)S(1)}, u32[]{:S(2)}, u32[]{:S(2)}) collective-permute-start(f32[64,256]{1,0:T(8,128)} %conv_deep.1), channel_id=1, source_target_pairs={{0,8},{1,9},{2,10},{3,11},{4,12},{5,13},{6,14},{7,15},{8,0},{9,1},... | collective-permute-start | bytes 196616 | tf_op jit(solution)/shard_map/ppermute | solution.py:384
  135.2 6.7 %collective-permute-start.26 = (f32[256,256]{1,0:T(8,128)S(1)}, f32[256,256]{1,0:T(8,128)S(1)}, u32[]{:S(2)}, u32[]{:S(2)}) collective-permute-start(f32[256,256]{1,0:T(8,128)S(1)} %pad_maximum_fusion.4), channel_id=1, source_target_pairs={{0,2},{1,3},{2,0},{3,1},{4,6},{5,7},{6,4},{7,5},{8,10},{9,11},{10,... | collective-permute-start | bytes 786440 | tf_op jit(solution)/shard_map/ppermute | solution.py:384
  (27 other events, 174.3 us)

commit v2 on v1

v2 whole, which is shorter than its diff:
```python
import functools

import jax
import jax.numpy as jnp
import numpy as np
from jax import lax
from jax.experimental import pallas as pl
from jax.experimental.pallas import tpu as pltpu
from jax.sharding import PartitionSpec as P


YA = 32
ZA = 16
MID_ROWS, MID_COLS = YA // 2, ZA // 2
MID_CELLS = MID_ROWS * MID_COLS
DEEP_ROWS, DEEP_COLS = YA // 4, ZA // 4
DEEP_CELLS = DEEP_ROWS * DEEP_COLS
LANES = 128
PACK = LANES // DEEP_CELLS
SMEM = pl.BlockSpec(memory_space=pltpu.SMEM)
VMEM = pl.BlockSpec(memory_space=pltpu.VMEM)


def grant(mebibytes):
    return pltpu.CompilerParams(vmem_limit_bytes=int(mebibytes * 1024 * 1024))


def split_outside(weights):
    rounded = lax.reduce_precision(weights, 8, 7)
    return rounded.astype(jnp.bfloat16), (weights - rounded).astype(jnp.bfloat16)


def split_inside(values):
    high = values.astype(jnp.bfloat16)
    return high, (values - high.astype(jnp.float32)).astype(jnp.bfloat16)


def product(left, right):
    return jnp.dot(left, right, preferred_element_type=jnp.float32)


def product_three(left_high, left_low, right_high, right_low):
    return (
        product(left_high, right_high)
        + product(left_high, right_low)
        + product(left_low, right_high)
    )


def product_stacked(left_high, left_low, right_high, right_low):
    count = left_high.shape[0]
    both = product(jnp.concatenate([left_high, left_low], axis=0), right_high)
    return both[:count] + both[count:] + product(left_high, right_low)


def picker(blocks, rows, cols, xp=jnp):
    small_rows, small_cols = rows // 2, cols // 2
    big = xp.arange(blocks * rows * cols)[:, None]
    small = xp.arange(4 * blocks * small_rows * small_cols)[None, :]
    cells = small_rows * small_cols
    tap, block, cell = small // (blocks * cells), small // cells % blocks, small % cells
    row = 2 * (cell // small_cols) + tap // 2
    col = 2 * (cell % small_cols) + tap % 2
    return (big == (block * rows + row) * cols + col).astype(jnp.bfloat16)


def inside(places, limit, step):
    moved = places + step
    return (moved >= 0) & (moved < limit)


def down_fine_kernel(field_ref, place_ref, weight_ref, out_ref, total_ref):
    step = pl.program_id(0)
    for a in range(2):

        @pl.when(step == a)
        def _():
            high, low = [
                lax.dot_general(
                    place_ref[...], part, (((1,), (1,)), ((), ())), preferred_element_type=jnp.float32
                ).astype(jnp.bfloat16)
                for part in split_inside(field_ref[:, a, :])
            ]
            total = jnp.zeros(total_ref.shape, jnp.float32) if a == 0 else total_ref[...]
            for tap in range(4):
                weight_high, weight_low = split_inside(weight_ref[tap])
                block = slice(tap * MID_CELLS, (tap + 1) * MID_CELLS)
                total = total + product_stacked(high[block], low[block], weight_high, weight_low)
            if a == 0:
                total_ref[...] = total
            else:
                out_ref[...] = total.T


def down_fine(field, place, weights):
    chan_fine, chan_mid = weights.shape[1:]
    return pl.pallas_call(
        down_fine_kernel,
        out_shape=jax.ShapeDtypeStruct((chan_mid, MID_CELLS), jnp.float32),
        grid=(2,),
        in_specs=[
            pl.BlockSpec(field.shape, lambda a: (0, 0, 0)),
            pl.BlockSpec(place.shape, lambda a: (0, 0)),
            pl.BlockSpec((4, chan_fine, chan_mid), lambda a: (a, 0, 0)),
        ],
        out_specs=pl.BlockSpec((chan_mid, MID_CELLS), lambda a: (0, 0)),
        scratch_shapes=[pltpu.VMEM((MID_CELLS, chan_mid), jnp.float32)],
        name="down_fine",
        compiler_params=grant(60),
    )(field, place, weights)


def plane_at(me, step, other, chips):
    chip, core = me // 2, me % 2
    step = jnp.where(core == 0, -step, step)
    position = jnp.where(chip % 2 == 0, chip // 2, chips - 1 - chip // 2)
    position = (position + step + chips) % chips
    chip = jnp.where(position < chips // 2, 2 * position, 2 * (chips - 1 - position) + 1)
    return 2 * chip + (1 - core if other else core)


def conv_mid_add(me, chips, places, high_ref, low_ref, fields, sum_ref):
    rows = sum_ref.shape[1]
    field_high, field_low = split_inside(jnp.concatenate(fields, axis=1))
    place = lax.broadcasted_iota(jnp.int32, (rows, LANES), 1)
    row_of, col_of = place // MID_COLS, place % MID_COLS
    for a in range(3):
        block = pl.ds(a * 9 * rows, 9 * rows)
        spread = product_three(high_ref[block, :], low_ref[block, :], field_high, field_low)
        for side, (step, other) in enumerate(places):
            total = jnp.zeros((rows, LANES), jnp.float32)
            for b in range(3):
                for c in range(3):
                    tap = 3 * b + c
                    piece = spread[tap * rows : (tap + 1) * rows, side * LANES : (side + 1) * LANES]
                    offset = (b - 1) * MID_COLS + (c - 1)
                    if offset:
                        piece = pltpu.roll(piece, (-offset) % LANES, 1)
                        keep = inside(row_of, MID_ROWS, b - 1) & inside(col_of, MID_COLS, c - 1)
                        piece = jnp.where(keep, piece, 0.0)
                    total = total + piece
            plane = plane_at(me, step, other, chips) + (2 - a)
            sum_ref[plane] = sum_ref[plane] + total


def conv_mid_kernel(chips, places, first, me_ref, high_ref, low_ref, *refs):
    sum_ref, both_ref = refs[-2:]
    if first:
        sum_ref[...] = jnp.zeros_like(sum_ref)
    else:
        sum_ref[...] = refs[-3][...]
    fields, at = [], 0
    while len(fields) < len(places):
        field = refs[at][...]
        fields += [field] if field.shape[1] == LANES else [field[:, :LANES], field[:, LANES:]]
        at += 1
    both_ref[...] = jnp.concatenate(fields[-2:], axis=1)
    conv_mid_add(me_ref[0], chips, places, high_ref, low_ref, fields, sum_ref)


def conv_mid(me, high, low, fields, places, running, planes):
    rows = high.shape[0] // 27
    arrays = [me, high, low, *fields] + ([] if running is None else [running])
    return pl.pallas_call(
        functools.partial(conv_mid_kernel, planes // 2, places, running is None),
        out_shape=(
            jax.ShapeDtypeStruct((planes + 2, rows, LANES), jnp.float32),
            jax.ShapeDtypeStruct((high.shape[1], 2 * LANES), jnp.float32),
        ),
        in_specs=[SMEM] + [VMEM] * (len(arrays) - 1),
        out_specs=(VMEM, VMEM),
        input_output_aliases={} if running is None else {len(arrays) - 1: 0},
        name="conv_mid",
        compiler_params=grant(14),
    )(*arrays)


def down_mid_kernel(chips, places, me_ref, high_ref, low_ref, pick_ref, weight_ref, *refs):
    running_ref, mid_ref, keep_ref, send_ref, sum_ref, turned, weight_high, weight_low = refs[-8:]
    turned[...] = weight_ref[...].T
    sorted_split(me_ref[0], [turned], weight_high, weight_low, chips, False)
    sum_ref[...] = running_ref[...]
    fields = [refs[0][:, :LANES], refs[0][:, LANES:], refs[1][...], refs[2][...]]
    conv_mid_add(me_ref[0], chips, places, high_ref, low_ref, fields, sum_ref)
    planes = mid_ref.shape[0]
    groups = planes // 2 // PACK
    mid_ref[...] = jnp.maximum(sum_ref[1 : planes + 1], 0.0)
    rows = mid_ref.shape[1]
    lines = []
    for a in range(2):
        for g in range(groups):
            lines.append(jnp.concatenate([mid_ref[2 * (g * PACK + q) + a] for q in range(PACK)], axis=1))
    high, low = split_inside(jnp.concatenate(lines, axis=0))
    picks = []
    for part in (high, low):
        moved = product(part, pick_ref[...]).astype(jnp.bfloat16)
        taps = []
        for a in range(2):
            for tap in range(4):
                taps.append(
                    jnp.concatenate(
                        [
                            moved[(a * groups + g) * rows : (a * groups + g + 1) * rows, tap * LANES : (tap + 1) * LANES]
                            for g in range(groups)
                        ],
                        axis=1,
                    )
                )
        picks.append(jnp.concatenate(taps, axis=0))
    half = keep_ref.shape[0]
    part = product_three(weight_high[...], weight_low[...], picks[0], picks[1])
    keep_ref[...] = part[:half]
    send_ref[...] = part[half:]


def down_mid(me, high, low, pick, weight, fields, places, running, planes):
    rows = high.shape[0] // 27
    arrays = [me, high, low, pick, weight, *fields, running]
    half = jax.ShapeDtypeStruct((weight.shape[1] // 2, planes // 2 * DEEP_CELLS), jnp.float32)
    turned = (weight.shape[1], weight.shape[0])
    return pl.pallas_call(
        functools.partial(down_mid_kernel, planes // 2, places),
        out_shape=(jax.ShapeDtypeStruct((planes, rows, LANES), jnp.float32), half, half),
        in_specs=[SMEM] + [VMEM] * (len(arrays) - 1),
        out_specs=(VMEM, VMEM, VMEM),
        scratch_shapes=[pltpu.VMEM(running.shape, jnp.float32), pltpu.VMEM(turned, jnp.float32)]
        + [pltpu.VMEM(turned, jnp.bfloat16)] * 2,
        name="down_mid",
        compiler_params=grant(16),
    )(*arrays)


def reversed_bits(value, blocks):
    width = blocks.bit_length() - 1
    return sum(((value >> k) & 1) << (width - 1 - k) for k in range(width))


def sorted_split(me, pieces, high_ref, low_ref, blocks, whole):
    size = sum(piece.shape[0] for piece in pieces) // blocks
    at = 0
    for piece in pieces:
        for line in range(piece.shape[0] // size):
            high, low = split_inside(piece[pl.ds(line * size, size), :])
            target = reversed_bits(at, blocks) ^ me if whole else at ^ reversed_bits(me % blocks, blocks)
            target = pl.ds(pl.multiple_of(target * size, size), size)
            high_ref[target, :] = high
            low_ref[target, :] = low
            at += 1


def conv_deep_kernel(blocks, me_ref, high_ref, low_ref, near_ref, far_ref, out_ref, field_high, field_low):
    sorted_split(me_ref[0], [near_ref, far_ref], field_high, field_low, blocks, False)
    rows, cells = out_ref.shape
    place = lax.broadcasted_iota(jnp.int32, (rows, cells), 1)
    plane_of = place // DEEP_CELLS
    row_of, col_of = place // DEEP_COLS % DEEP_ROWS, place % DEEP_COLS
    summed = jnp.zeros((rows, cells), jnp.float32)
    for a in range(3):
        block = pl.ds(a * 9 * rows, 9 * rows)
        spread = product_three(high_ref[block, :], low_ref[block, :], field_high[...], field_low[...])
        total = jnp.zeros((rows, cells), jnp.float32)
        for b in range(3):
            for c in range(3):
                tap = 3 * b + c
                piece = spread[tap * rows : (tap + 1) * rows]
                offset = (b - 1) * DEEP_COLS + (c - 1)
                if offset:
                    piece = pltpu.roll(piece, (-offset) % cells, 1)
                    keep = inside(row_of, DEEP_ROWS, b - 1) & inside(col_of, DEEP_COLS, c - 1)
                    piece = jnp.where(keep, piece, 0.0)
                total = total + piece
        if a != 1:
            total = pltpu.roll(total, (-(a - 1) * DEEP_CELLS) % cells, 1)
            total = jnp.where(inside(plane_of, cells // DEEP_CELLS, a - 1), total, 0.0)
        summed = summed + total
    out_ref[...] = jnp.maximum(summed, 0.0)


def conv_deep(me, blocks, high, low, near, far):
    rows, cells = high.shape[0] // 27, near.shape[1]
    return pl.pallas_call(
        functools.partial(conv_deep_kernel, blocks),
        out_shape=jax.ShapeDtypeStruct((rows, cells), jnp.float32),
        in_specs=[SMEM] + [VMEM] * 4,
        out_specs=VMEM,
        scratch_shapes=[pltpu.VMEM((high.shape[1], cells), jnp.bfloat16)] * 2,
        name="conv_deep",
        compiler_params=grant(16),
    )(me, high, low, near, far)


def up_deep_kernel(blocks, me_ref, turn_ref, first_ref, second_ref, *refs):
    near_ref, far_ref, place_ref, mid_ref, out_ref, field_high, field_low = refs
    sorted_split(me_ref[0], [near_ref, far_ref], field_high, field_low, blocks, True)
    flip = turn_ref[0] != 0
    upper = jnp.where(flip, second_ref[...], first_ref[...])
    lower = jnp.where(flip, first_ref[...], second_ref[...])
    weight_rows = jnp.concatenate([upper, lower], axis=1)
    planes, rows, _ = mid_ref.shape
    groups = planes // 2 // PACK
    size = weight_rows.shape[2] // 8
    weight = jnp.concatenate(
        [
            jnp.concatenate([weight_rows[block, :, tap * size : (tap + 1) * size] for block in range(blocks)], axis=1)
            for tap in range(8)
        ],
        axis=0,
    )
    weight_high, weight_low = split_inside(weight)
    spread = product_three(weight_high, weight_low, field_high[...], field_low[...])
    lines = []
    for a in range(2):
        for g in range(groups):
            lines.append(
                jnp.concatenate(
                    [
                        spread[(4 * a + tap) * rows : (4 * a + tap + 1) * rows, g * LANES : (g + 1) * LANES]
                        for tap in range(4)
                    ],
                    axis=1,
                )
            )
    high, low = split_inside(jnp.concatenate(lines, axis=0))
    lifted = product(high, place_ref[...]) + product(low, place_ref[...])
    for a in range(2):
        for g in range(groups):
            for q in range(PACK):
                plane = 2 * (g * PACK + q) + a
                line = (a * groups + g) * rows
                piece = lifted[line : line + rows, q * LANES : (q + 1) * LANES]
                out_ref[plane] = jnp.maximum(mid_ref[plane] + piece, 0.0)


def up_deep(me, turn, blocks, first, second, near, far, place, mid):
    depth, cells = 2 * near.shape[0], near.shape[1]
    return pl.pallas_call(
        functools.partial(up_deep_kernel, blocks),
        out_shape=jax.ShapeDtypeStruct(mid.shape, jnp.float32),
        in_specs=[SMEM] * 2 + [VMEM] * 6,
        out_specs=VMEM,
        scratch_shapes=[pltpu.VMEM((depth, cells), jnp.bfloat16)] * 2,
        name="up_deep",
        compiler_params=grant(16),
    )(me, turn, first, second, near, far, place, mid)


def up_mid_kernel(high_ref, low_ref, field_ref, place_ref, out_ref):
    field_high, field_low = split_inside(field_ref[...].reshape(-1, LANES).T)
    for a in range(2):
        lines = [
            product_stacked(field_high, field_low, high_ref[4 * a + tap], low_ref[4 * a + tap]) for tap in range(4)
        ]
        high, low = split_inside(jnp.concatenate(lines, axis=0).T)
        out_ref[:, a, :] = product(high, place_ref[...]) + product(low, place_ref[...])


def up_mid(high, low, field, place):
    return pl.pallas_call(
        up_mid_kernel,
        out_shape=jax.ShapeDtypeStruct((high.shape[2], 2, place.shape[1]), jnp.float32),
        in_specs=[VMEM] * 4,
        out_specs=VMEM,
        name="up_mid",
        compiler_params=grant(16),
    )(high, low, field, place)


def turn_rows_kernel(turn_ref, weight_ref, out_ref):
    count, half, depth = out_ref.shape
    turned = weight_ref[...].T.reshape(count, 2, half, depth)
    out_ref[...] = jnp.where(turn_ref[0] != 0, turned[:, 1], turned[:, 0])


def turn_rows(turn, weight, count):
    depth, chan = weight.shape
    return pl.pallas_call(
        turn_rows_kernel,
        out_shape=jax.ShapeDtypeStruct((count, chan // count // 2, depth), jnp.float32),
        in_specs=[SMEM, VMEM],
        out_specs=VMEM,
        name="turn_rows",
        compiler_params=grant(8),
    )(turn, weight)


def join_kernel(near_ref, far_ref, out_ref):
    half = near_ref.shape[0]
    out_ref[:half] = near_ref[...]
    out_ref[half:] = far_ref[...]


def join(near, far):
    return pl.pallas_call(
        join_kernel,
        out_shape=jax.ShapeDtypeStruct((2 * near.shape[0], near.shape[1]), jnp.float32),
        in_specs=[VMEM] * 2,
        out_specs=VMEM,
        name="join",
        compiler_params=grant(4),
    )(near, far)


def swap(field, bit):
    count = lax.axis_size("wide")
    return lax.ppermute(field, "wide", [(i, i ^ bit) for i in range(count)])


def shards(fine_field, w_down_fine, w_conv_mid, w_down_mid, w_conv_deep, w_up_deep, w_up_mid):
    count = lax.axis_size("wide")
    me = lax.axis_index("wide")
    me_array = me.astype(jnp.int32).reshape(1)
    chips = count // 2
    bits = [1 << k for k in range(count.bit_length() - 1)]
    mid_local, chan_mid = w_conv_mid.shape[1:]
    deep_local, chan_deep = w_conv_deep.shape[1:]
    place_fine = jnp.asarray(picker(1, YA, ZA, np).T)
    pick_mid = picker(PACK, MID_ROWS, MID_COLS)

    mid_input = down_fine(fine_field, place_fine, w_down_fine)

    conv_high, conv_low = split_outside(w_conv_mid.reshape(27 * mid_local, chan_mid))
    down_weight = w_down_mid.reshape(8 * mid_local, chan_deep)
    turn_array = (lax.axis_index("groups") % 2).astype(jnp.int32).reshape(1)
    w_half = turn_rows(turn_array, w_up_deep.reshape(8 * deep_local, chan_mid), count)

    ring = list(range(0, chips, 2)) + list(range(chips - 1, 0, -2))
    links = [(2 * ring[k], 2 * ring[(k + 1) % chips]) for k in range(chips)]
    links += [(2 * ring[(k + 1) % chips] + 1, 2 * ring[k] + 1) for k in range(chips)]
    steps = chips // 2
    near, far = mid_input, swap(mid_input, 1)
    running = None
    fields, places = [near, far], [(0, False), (0, True)]
    for step in range(1, steps + 1):
        near = lax.ppermute(near, "wide", links)
        if step < steps:
            far = lax.ppermute(far, "wide", links)
        if step == 1:
            near, conv_high, conv_low = lax.optimization_barrier((near, conv_high, conv_low))
        else:
            running, both = conv_mid(me_array, conv_high, conv_low, fields, places, running, count)
            near, running = lax.optimization_barrier((near, running))
            fields, places = [swap(both, 1)], [(1 - step, True), (1 - step, False)]
        fields.append(near)
        places.append((step, False))
        if step < steps:
            fields.append(far)
            places.append((step, True))
    fields.append(swap(near, 1))
    places.append((-steps, True))
    mid_field, keep, send = down_mid(
        me_array, conv_high, conv_low, pick_mid, down_weight, fields, places, running, count
    )

    deep_high, deep_low = split_outside(w_conv_deep.reshape(27 * deep_local, chan_deep))
    held = keep + swap(send, 1)
    for bit in bits[1:-1]:
        size = held.shape[0] // 2
        held = held[:size] + swap(held[size:], bit)
        if bit == bits[1]:
            held, deep_high, deep_low = lax.optimization_barrier((held, deep_high, deep_low))
    held = jax.nn.relu(held + swap(held, bits[-1]))
    held, w_half = lax.optimization_barrier((held, w_half))
    for bit in bits[-2:0:-1]:
        held = join(held, swap(held, bit))
    w_near = lax.all_to_all(w_half, "wide", split_axis=0, concat_axis=0, tiled=True)
    deep_output = conv_deep(me_array, count // 2, deep_high, deep_low, held, swap(held, 1))

    deep_output, w_near = lax.optimization_barrier((deep_output, w_near))
    pairs = [(i, i ^ 1) for i in range(lax.axis_size("groups"))]
    w_far = lax.ppermute(w_near, "groups", pairs)
    last_high, last_low = split_outside(w_up_mid)
    held = deep_output
    for bit in bits[:0:-1]:
        held = join(held, swap(held, bit))
        if bit == bits[1]:
            held, last_high, last_low = lax.optimization_barrier((held, last_high, last_low))
    other = swap(held, 1)
    merged = up_deep(me_array, turn_array, count, w_near, w_far, held, other, pick_mid.T, mid_field)

    plane = lax.all_to_all(merged, "wide", split_axis=0, concat_axis=0, tiled=True)
    return up_mid(last_high, last_low, plane, place_fine)


def solution(mesh):
    return jax.shard_map(
        shards,
        mesh=mesh,
        in_specs=(
            P(None, ("groups", "wide"), None),
            P(),
            P(None, "wide", None),
            P(None, "wide", None),
            P(None, "wide", None),
            P(None, "wide", None),
            P(),
        ),
        out_specs=P(None, ("groups", "wide"), None),
        check_vma=False,
    )
```

time: 170 us -> 159 us (0.935)
  Pallas kernels: 41.6 us -> 24.5 us
  starting transfers between devices: 25.9 us -> 37.3 us
  waiting for transfers between devices: 70.5 us -> 67.3 us
    ppermute x20 -> x16, waiting for transfers between devices: 58.7 us -> 40.9 us  [swap(): return lax.ppermute(field, 'wide', [(i, i ^ bit) for i in range(count)])]
    ppermute x8, waiting for transfers between devices: 11.8 us -> 26.4 us  [the longest x1 10.2 us: shards(): w_far = lax.ppermute(w_near, 'groups', pairs)]
    pallas_call x5 -> x11, Pallas kernels: 23.6 us -> 11.3 us  [the longest x3 5.39 us: conv_mid(): pl.pallas_call(functools.partial(conv_mid_kernel, planes // 2, places, ru...]
    ppermute x8, starting transfers between devices: 9.47 us -> 15.1 us  [the longest x4 8.69 us: shards(): near = lax.ppermute(near, 'wide', links)]
    convert_element_type x1 -> x3, other arithmetic: 1.43 us -> 6.54 us  [split_outside(): (weights - rounded).astype(jnp.bfloat16)]
    ppermute x20 -> x16, starting transfers between devices: 12.3 us -> 16.3 us  [swap(): return lax.ppermute(field, 'wide', [(i, i ^ bit) for i in range(count)])]
    concatenate x6 -> x0, other arithmetic: 3.69 us -> none  [shards(): held = jnp.concatenate([held, swap(held, bit)], axis=0)]
    pallas_call x1, Pallas kernels: 6.83 us -> 3.34 us  [conv_deep(): pl.pallas_call(functools.partial(conv_deep_kernel, blocks), out_shape=jax...]
  transfers between devices with their start and end apart: 29 -> 25, of which waited for: 15 -> 19; matrix products, arithmetic and copies ran while one was open for 5% -> 5% of each run, Pallas kernels for 11% -> 4%
where the time goes in v2:
time: 159 us; the launch traced here: 158 us
  waiting for transfers between devices  67.3 us (42%)
  starting transfers between devices  37.3 us (23%)
  Pallas kernels  24.5 us (15%)
  blocking collectives  12.6 us (8%)
  other arithmetic  9.96 us (6%)
  local copies, waits for them, and re-layouts  6.46 us (4%)
    ppermute x16, waiting for transfers between devices, swap(): return lax.ppermute(field, 'wide', [(i, i ^ bit) for i in range(count)])  40.9 us
    ppermute x16, starting transfers between devices, swap(): return lax.ppermute(field, 'wide', [(i, i ^ bit) for i in range(count)])  16.3 us
    all_to_all x1, blocking collectives, shards(): lax.all_to_all(merged, 'wide', split_axis=0, concat_axis=0, tiled=True)  12.6 us
    ppermute x1, waiting for transfers between devices, shards(): w_far = lax.ppermute(w_near, 'groups', pairs)  10.2 us
    ppermute x4, waiting for transfers between devices, shards(): near = lax.ppermute(near, 'wide', links)  9.83 us
    ppermute x4, starting transfers between devices, shards(): near = lax.ppermute(near, 'wide', links)  8.69 us
    pallas_call x1, Pallas kernels, down_fine(): pl.pallas_call(down_fine_kernel, out_shape=jax.ShapeDtypeStruct((chan_mid...  7.61 us
    convert_element_type x3, other arithmetic, split_outside(): (weights - rounded).astype(jnp.bfloat16)  6.54 us
  transfers between devices with their start and end apart: 25, of which 19 were waited for; matrix products, arithmetic and copies ran while one was open for 5% of the time, Pallas kernels for 4%

profile of v2, /device:TPU:0, one launch (start us, length us, event | category | flops | bytes accessed | tf_op | source)
XLA Modules:
  0.0 158.4 jit_solution(2660892462229188945)
XLA Ops:
  0.0 7.6 %down_fine.1.refs_0_ = f32[512,128]{1,0:T(8,128)} custom-call(f32[256,2,512]{2,1,0:T(2,128)} %field_ref.1, bf16[512,512]{1,0:T(8,128)(2,1)} %constant.111.clone.place_ref, f32[8,256,512]{2,1,0:T(8,128)} %weight_ref.1), custom_call_target="tpu_custom_call" | custom-call | tf_op jit(solution)/shard_map/down_fine/pallas_call | solution.py:97
  8.1 2.6 %collective-permute-start = (f32[512,128]{1,0:T(8,128)}, f32[512,128]{1,0:T(8,128)S(1)}, u32[]{:S(2)}, u32[]{:S(2)}) collective-permute-start(f32[512,128]{1,0:T(8,128)} %down_fine.1.refs_0_), channel_id=1, source_target_pairs={{0,4},{4,8},{8,12},{12,14},{14,10},{10,6},{6,2},{2,0},{5,1},{9,5},... | collective-permute-start | bytes 786440 | tf_op jit(solution)/shard_map/ppermute | solution.py:434
  12.7 2.6 %collective-permute-done.refs_2_ = f32[512,128]{1,0:T(8,128)S(1)} collective-permute-done((f32[512,128]{1,0:T(8,128)}, f32[512,128]{1,0:T(8,128)S(1)}, u32[]{:S(2)}, u32[]{:S(2)}) %collective-permute-start) | collective-permute-done | bytes 262176 | tf_op jit(solution)/shard_map/ppermute | solution.py:434
  15.2 2.8 %collective-permute-done.2.refs_3_ = f32[512,128]{1,0:T(8,128)S(1)} collective-permute-done((f32[512,128]{1,0:T(8,128)S(1)}, f32[512,128]{1,0:T(8,128)S(1)}, u32[]{:S(2)}, u32[]{:S(2)}) %collective-permute-start.2) | collective-permute-done | bytes 262176 | tf_op jit(solution)/shard_map/ppermute | solution.py:436
  23.6 2.8 %collective-permute-done.4.refs_1_ = f32[512,128]{1,0:T(8,128)S(1)} collective-permute-done((f32[512,128]{1,0:T(8,128)S(1)}, f32[512,128]{1,0:T(8,128)S(1)}, u32[]{:S(2)}, u32[]{:S(2)}) %collective-permute-start.4) | collective-permute-done | bytes 262176 | tf_op jit(solution)/shard_map/ppermute | solution.py:434
  26.3 2.8 %collective-permute-done.5.refs_2_ = f32[512,128]{1,0:T(8,128)S(1)} collective-permute-done((f32[512,128]{1,0:T(8,128)S(1)}, f32[512,128]{1,0:T(8,128)S(1)}, u32[]{:S(2)}, u32[]{:S(2)}) %collective-permute-start.5) | collective-permute-done | bytes 262176 | tf_op jit(solution)/shard_map/ppermute | solution.py:436
  34.7 2.8 %collective-permute-done.7.refs_1_ = f32[512,128]{1,0:T(8,128)S(1)} collective-permute-done((f32[512,128]{1,0:T(8,128)S(1)}, f32[512,128]{1,0:T(8,128)S(1)}, u32[]{:S(2)}, u32[]{:S(2)}) %collective-permute-start.7) | collective-permute-done | bytes 262176 | tf_op jit(solution)/shard_map/ppermute | solution.py:434
  45.4 2.6 %down_mid.1 = (f32[16,32,128]{2,1,0:T(8,128)S(1)}, f32[512,256]{1,0:T(8,128)S(1)}, f32[512,256]{1,0:T(8,128)S(1)}) custom-call(s32[1]{0:T(128)} %bitcast.me_ref, bf16[864,512]{1,0:T(8,128)(2,1)S(1)} %get-tuple-element.33.high_ref, bf16[864,512]{1,0:T(8,128)(2,1)S(1)} %get-tuple-element.34.low_ref, bf16[512,512]{1,0:T(8,128)(2,1)S(1)} %get-tuple-element.68.pick_ref, ...), custom_call_target="tpu_custom_call" | custom-call | tf_op jit(solution)/shard_map/down_mid/pallas_call | solution.py:221
  52.2 3.4 %fusion = (bf16[1728,1024]{1,0:T(8,128)(2,1)S(1)}, bf16[1728,1024]{1,0:T(8,128)(2,1)}) fusion(f32[27,64,1024]{2,1,0:T(8,128)S(1)} %bitcast.13), kind=kLoop, calls=%fused_computation.2 | loop fusion | flops 7077888 | bytes 14155776 | tf_op jit(solution)/shard_map/convert_element_type | solution.py:30
  55.5 3.2 %collective-permute-done.13 = f32[256,256]{1,0:T(8,128)S(1)} collective-permute-done((f32[256,256]{1,0:T(8,128)S(1)}, f32[256,256]{1,0:T(8,128)S(1)}, u32[]{:S(2)}, u32[]{:S(2)}) %collective-permute-start.13) | collective-permute-done | bytes 262176 | tf_op jit(solution)/shard_map/ppermute | solution.py:405
  60.7 3.2 %collective-permute-done.14 = f32[128,256]{1,0:T(8,128)S(1)} collective-permute-done((f32[128,256]{1,0:T(8,128)S(1)}, f32[128,256]{1,0:T(8,128)S(1)}, u32[]{:S(2)}, u32[]{:S(2)}) %collective-permute-start.14) | collective-permute-done | bytes 131104 | tf_op jit(solution)/shard_map/ppermute | solution.py:405
  64.5 2.8 %collective-permute-start.15 = (f32[128,256]{1,0:T(8,128)}, f32[128,256]{1,0:T(8,128)}, u32[]{:S(2)}, u32[]{:S(2)}) collective-permute-start(f32[128,256]{1,0:T(8,128)} %slice_add_fusion.1), channel_id=1, source_target_pairs={{0,8},{1,9},{2,10},{3,11},{4,12},{5,13},{6,14},{7,15},{8,0},{9,1},... | collective-permute-start | bytes 393224 | tf_op jit(solution)/shard_map/ppermute | solution.py:405
  69.7 2.6 %collective-permute-done.15 = f32[128,256]{1,0:T(8,128)} collective-permute-done((f32[128,256]{1,0:T(8,128)}, f32[128,256]{1,0:T(8,128)}, u32[]{:S(2)}, u32[]{:S(2)}) %collective-permute-start.15) | collective-permute-done | bytes 131104 | tf_op jit(solution)/shard_map/ppermute | solution.py:405
  74.0 5.9 %all-to-all-start = ((f32[16,16,512]{2,1,0:T(8,128)}), f32[16,16,512]{2,1,0:T(8,128)}, u32[]{:S(2)}, u32[]{:S(2)}) async-start(f32[16,16,512]{2,1,0:T(8,128)} %copy-done.2), calls=%async_computation | async-start | bytes 1048576 | tf_op jit(solution)/shard_map/all_to_all | solution.py:465
  81.8 12.3 %collective-permute-done.16.far_ref = f32[128,256]{1,0:T(8,128)S(1)} collective-permute-done((f32[128,256]{1,0:T(8,128)}, f32[128,256]{1,0:T(8,128)S(1)}, u32[]{:S(2)}, u32[]{:S(2)}) %collective-permute-start.16) | collective-permute-done | bytes 131104 | tf_op jit(solution)/shard_map/ppermute | solution.py:405
  96.5 5.5 %collective-permute-done.17.far_ref = f32[256,256]{1,0:T(8,128)S(1)} collective-permute-done((f32[256,256]{1,0:T(8,128)S(1)}, f32[256,256]{1,0:T(8,128)S(1)}, u32[]{:S(2)}, u32[]{:S(2)}) %collective-permute-start.17) | collective-permute-done | bytes 262176 | tf_op jit(solution)/shard_map/ppermute | solution.py:405
  106.0 3.3 %conv_deep.1.near_ref = f32[64,256]{1,0:T(8,128)S(1)} custom-call(s32[1]{0:T(128)} %bitcast.me_ref, bf16[1728,1024]{1,0:T(8,128)(2,1)S(1)} %copy-done, bf16[1728,1024]{1,0:T(8,128)(2,1)S(1)} %get-tuple-element.51.low_ref, f32[512,256]{1,0:T(8,128)S(1)} %join.6.near_ref, f32[512,256]{1,0:T(8,128)S(1)} %collective-permute-done.18.far_ref), custom_call_target="tpu_custom_call" | custom-call | tf_op jit(solution)/shard_map/conv_deep/pallas_call | solution.py:281
  110.0 3.3 %collective-permute-start.19 = (f32[64,256]{1,0:T(8,128)}, f32[64,256]{1,0:T(8,128)S(1)}, u32[]{:S(2)}, u32[]{:S(2)}) collective-permute-start(f32[64,256]{1,0:T(8,128)} %copy-done.8), channel_id=1, source_target_pairs={{0,8},{1,9},{2,10},{3,11},{4,12},{5,13},{6,14},{7,15},{8,0},{9,1},... | collective-permute-start | bytes 196616 | tf_op jit(solution)/shard_map/ppermute | solution.py:405
  113.3 4.0 %collective-permute-done.19.far_ref = f32[64,256]{1,0:T(8,128)S(1)} collective-permute-done((f32[64,256]{1,0:T(8,128)}, f32[64,256]{1,0:T(8,128)S(1)}, u32[]{:S(2)}, u32[]{:S(2)}) %collective-permute-start.19) | collective-permute-done | bytes 65568 | tf_op jit(solution)/shard_map/ppermute | solution.py:405
  118.2 5.0 %collective-permute-done.20.far_ref = f32[128,256]{1,0:T(8,128)S(1)} collective-permute-done((f32[128,256]{1,0:T(8,128)S(1)}, f32[128,256]{1,0:T(8,128)S(1)}, u32[]{:S(2)}, u32[]{:S(2)}) %collective-permute-start.20) | collective-permute-done | bytes 131104 | tf_op jit(solution)/shard_map/ppermute | solution.py:405
  125.0 2.9 %fusion.1 = (bf16[8,512,256]{2,1,0:T(8,128)(2,1)S(1)}, bf16[8,512,256]{2,1,0:T(8,128)(2,1)S(1)}) fusion(f32[8,512,256]{2,1,0:T(8,128)} %param.14), kind=kLoop, calls=%fused_computation.5 | loop fusion | flops 4194304 | bytes 8388608 | tf_op jit(solution)/shard_map/convert_element_type | solution.py:30
  130.5 10.2 %collective-permute-done.22.second_ref = f32[16,16,512]{2,1,0:T(8,128)S(1)} collective-permute-done((f32[16,16,512]{2,1,0:T(8,128)}, f32[16,16,512]{2,1,0:T(8,128)S(1)}, u32[]{:S(2)}, u32[]{:S(2)}) %collective-permute-start.22) | collective-permute-done | bytes 524320 | tf_op jit(solution)/shard_map/ppermute | solution.py:470
  143.0 12.6 %all_to_all.10.field_ref = f32[16,32,128]{2,1,0:T(8,128)S(1)} all-to-all(f32[16,32,128]{2,1,0:T(8,128)S(1)} %up_deep.1), channel_id=1, replica_groups=mesh['groups'=2,'wide'=16] {'wide'}, dimensions={0} | all-to-all | bytes 524288 | tf_op jit(solution)/shard_map/all_to_all | solution.py:480
  155.6 2.8 %up_mid.1 = f32[256,2,512]{2,1,0:T(2,128)} custom-call(bf16[8,512,256]{2,1,0:T(8,128)(2,1)S(1)} %get-tuple-element.56.high_ref, bf16[8,512,256]{2,1,0:T(8,128)(2,1)S(1)} %get-tuple-element.57.low_ref, f32[16,32,128]{2,1,0:T(8,128)S(1)} %all_to_all.10.field_ref, bf16[512,512]{1,0:T(8,128)(2,1)S(1)} %copy-done.1), custom_call_target="tpu_custom_call" | custom-call | tf_op jit(solution)/shard_map/up_mid/pallas_call | solution.py:358
  (83 shorter events, 48.5 us)
Async XLA Ops:
  7.6 3.1 %collective-permute-start.1 = (f32[512,128]{1,0:T(8,128)}, f32[512,128]{1,0:T(8,128)S(1)}, u32[]{:S(2)}, u32[]{:S(2)}) collective-permute-start(f32[512,128]{1,0:T(8,128)} %down_fine.1.refs_0_), channel_id=1, source_target_pairs={{0,1},{1,0},{2,3},{3,2},{4,5},{5,4},{6,7},{7,6},{8,9},{9,8},{10,11... | collective-permute-start | bytes 786440 | tf_op jit(solution)/shard_map/ppermute | solution.py:405
  8.1 7.1 %collective-permute-start = (f32[512,128]{1,0:T(8,128)}, f32[512,128]{1,0:T(8,128)S(1)}, u32[]{:S(2)}, u32[]{:S(2)}) collective-permute-start(f32[512,128]{1,0:T(8,128)} %down_fine.1.refs_0_), channel_id=1, source_target_pairs={{0,4},{4,8},{8,12},{12,14},{14,10},{10,6},{6,2},{2,0},{5,1},{9,5},... | collective-permute-start | bytes 786440 | tf_op jit(solution)/shard_map/ppermute | solution.py:434
  10.7 7.4 %collective-permute-start.2 = (f32[512,128]{1,0:T(8,128)S(1)}, f32[512,128]{1,0:T(8,128)S(1)}, u32[]{:S(2)}, u32[]{:S(2)}) collective-permute-start(f32[512,128]{1,0:T(8,128)S(1)} %collective-permute-done.1.refs_1_), channel_id=1, source_target_pairs={{0,4},{4,8},{8,12},{12,14},{14,10},{10,6},{6,2},{2,0},{5,1},{9,5},... | collective-permute-start | bytes 786440 | tf_op jit(solution)/shard_map/ppermute | solution.py:436
  19.8 9.3 %collective-permute-start.3 = (f32[512,256]{1,0:T(8,128)S(1)}, f32[512,256]{1,0:T(8,128)S(1)}, u32[]{:S(2)}, u32[]{:S(2)}) collective-permute-start(f32[512,256]{1,0:T(8,128)S(1)} %get-tuple-element.36), channel_id=1, source_target_pairs={{0,1},{1,0},{2,3},{3,2},{4,5},{5,4},{6,7},{7,6},{8,9},{9,8},{10,11... | collective-permute-start | bytes 1572872 | tf_op jit(solution)/shard_map/ppermute | solution.py:405
  19.9 6.4 %collective-permute-start.4 = (f32[512,128]{1,0:T(8,128)S(1)}, f32[512,128]{1,0:T(8,128)S(1)}, u32[]{:S(2)}, u32[]{:S(2)}) collective-permute-start(f32[512,128]{1,0:T(8,128)S(1)} %collective-permute-done.refs_2_), channel_id=1, source_target_pairs={{0,4},{4,8},{8,12},{12,14},{14,10},{10,6},{6,2},{2,0},{5,1},{9,5},... | collective-permute-start | bytes 786440 | tf_op jit(solution)/shard_map/ppermute | solution.py:434
  22.0 7.2 %collective-permute-start.5 = (f32[512,128]{1,0:T(8,128)S(1)}, f32[512,128]{1,0:T(8,128)S(1)}, u32[]{:S(2)}, u32[]{:S(2)}) collective-permute-start(f32[512,128]{1,0:T(8,128)S(1)} %collective-permute-done.2.refs_3_), channel_id=1, source_target_pairs={{0,4},{4,8},{8,12},{12,14},{14,10},{10,6},{6,2},{2,0},{5,1},{9,5},... | collective-permute-start | bytes 786440 | tf_op jit(solution)/shard_map/ppermute | solution.py:436
  31.0 9.3 %collective-permute-start.6 = (f32[512,256]{1,0:T(8,128)S(1)}, f32[512,256]{1,0:T(8,128)S(1)}, u32[]{:S(2)}, u32[]{:S(2)}) collective-permute-start(f32[512,256]{1,0:T(8,128)S(1)} %get-tuple-element.40), channel_id=1, source_target_pairs={{0,1},{1,0},{2,3},{3,2},{4,5},{5,4},{6,7},{7,6},{8,9},{9,8},{10,11... | collective-permute-start | bytes 1572872 | tf_op jit(solution)/shard_map/ppermute | solution.py:405
  31.1 6.4 %collective-permute-start.7 = (f32[512,128]{1,0:T(8,128)S(1)}, f32[512,128]{1,0:T(8,128)S(1)}, u32[]{:S(2)}, u32[]{:S(2)}) collective-permute-start(f32[512,128]{1,0:T(8,128)S(1)} %collective-permute-done.4.refs_1_), channel_id=1, source_target_pairs={{0,4},{4,8},{8,12},{12,14},{14,10},{10,6},{6,2},{2,0},{5,1},{9,5},... | collective-permute-start | bytes 786440 | tf_op jit(solution)/shard_map/ppermute | solution.py:434
  33.1 7.2 %collective-permute-start.8 = (f32[512,128]{1,0:T(8,128)S(1)}, f32[512,128]{1,0:T(8,128)S(1)}, u32[]{:S(2)}, u32[]{:S(2)}) collective-permute-start(f32[512,128]{1,0:T(8,128)S(1)} %collective-permute-done.5.refs_2_), channel_id=1, source_target_pairs={{0,4},{4,8},{8,12},{12,14},{14,10},{10,6},{6,2},{2,0},{5,1},{9,5},... | collective-permute-start | bytes 786440 | tf_op jit(solution)/shard_map/ppermute | solution.py:436
  37.5 6.4 %collective-permute-start.10 = (f32[512,128]{1,0:T(8,128)S(1)}, f32[512,128]{1,0:T(8,128)S(1)}, u32[]{:S(2)}, u32[]{:S(2)}) collective-permute-start(f32[512,128]{1,0:T(8,128)S(1)} %collective-permute-done.7.refs_1_), channel_id=1, source_target_pairs={{0,4},{4,8},{8,12},{12,14},{14,10},{10,6},{6,2},{2,0},{5,1},{9,5},... | collective-permute-start | bytes 786440 | tf_op jit(solution)/shard_map/ppermute | solution.py:434
  42.1 3.3 %collective-permute-start.9 = (f32[512,256]{1,0:T(8,128)S(1)}, f32[512,256]{1,0:T(8,128)S(1)}, u32[]{:S(2)}, u32[]{:S(2)}) collective-permute-start(f32[512,256]{1,0:T(8,128)S(1)} %get-tuple-element.44), channel_id=1, source_target_pairs={{0,1},{1,0},{2,3},{3,2},{4,5},{5,4},{6,7},{7,6},{8,9},{9,8},{10,11... | collective-permute-start | bytes 1572872 | tf_op jit(solution)/shard_map/ppermute | solution.py:405
  48.0 2.0 %collective-permute-start.12 = (f32[512,256]{1,0:T(8,128)S(1)}, f32[512,256]{1,0:T(8,128)S(1)}, u32[]{:S(2)}, u32[]{:S(2)}) collective-permute-start(f32[512,256]{1,0:T(8,128)S(1)} %get-tuple-element.49), channel_id=1, source_target_pairs={{0,1},{1,0},{2,3},{3,2},{4,5},{5,4},{6,7},{7,6},{8,9},{9,8},{10,11... | collective-permute-start | bytes 1572872 | tf_op jit(solution)/shard_map/ppermute | solution.py:405
  50.1 8.6 %collective-permute-start.13 = (f32[256,256]{1,0:T(8,128)S(1)}, f32[256,256]{1,0:T(8,128)S(1)}, u32[]{:S(2)}, u32[]{:S(2)}) collective-permute-start(f32[256,256]{1,0:T(8,128)S(1)} %slice.17), channel_id=1, source_target_pairs={{0,2},{1,3},{2,0},{3,1},{4,6},{5,7},{6,4},{7,5},{8,10},{9,11},{10,... | collective-permute-start | bytes 786440 | tf_op jit(solution)/shard_map/ppermute | solution.py:405
  58.8 5.0 %collective-permute-start.14 = (f32[128,256]{1,0:T(8,128)S(1)}, f32[128,256]{1,0:T(8,128)S(1)}, u32[]{:S(2)}, u32[]{:S(2)}) collective-permute-start(f32[128,256]{1,0:T(8,128)S(1)} %slice.15), channel_id=1, source_target_pairs={{0,4},{1,5},{2,6},{3,7},{4,0},{5,1},{6,2},{7,3},{8,12},{9,13},{10,... | collective-permute-start | bytes 393224 | tf_op jit(solution)/shard_map/ppermute | solution.py:405
  64.5 7.8 %collective-permute-start.15 = (f32[128,256]{1,0:T(8,128)}, f32[128,256]{1,0:T(8,128)}, u32[]{:S(2)}, u32[]{:S(2)}) collective-permute-start(f32[128,256]{1,0:T(8,128)} %slice_add_fusion.1), channel_id=1, source_target_pairs={{0,8},{1,9},{2,10},{3,11},{4,12},{5,13},{6,14},{7,15},{8,0},{9,1},... | collective-permute-start | bytes 393224 | tf_op jit(solution)/shard_map/ppermute | solution.py:405
  74.0 36.0 %all-to-all-start = ((f32[16,16,512]{2,1,0:T(8,128)}), f32[16,16,512]{2,1,0:T(8,128)}, u32[]{:S(2)}, u32[]{:S(2)}) async-start(f32[16,16,512]{2,1,0:T(8,128)} %copy-done.2), calls=%async_computation | async-start | bytes 1048576 | tf_op jit(solution)/shard_map/all_to_all | solution.py:465
  79.9 14.2 %collective-permute-start.16 = (f32[128,256]{1,0:T(8,128)}, f32[128,256]{1,0:T(8,128)S(1)}, u32[]{:S(2)}, u32[]{:S(2)}) collective-permute-start(f32[128,256]{1,0:T(8,128)} %add_maximum_fusion.near_ref), channel_id=1, source_target_pairs={{0,4},{1,5},{2,6},{3,7},{4,0},{5,1},{6,2},{7,3},{8,12},{9,13},{10,... | collective-permute-start | bytes 393224 | tf_op jit(solution)/shard_map/ppermute | solution.py:405
  95.0 7.0 %collective-permute-start.17 = (f32[256,256]{1,0:T(8,128)S(1)}, f32[256,256]{1,0:T(8,128)S(1)}, u32[]{:S(2)}, u32[]{:S(2)}) collective-permute-start(f32[256,256]{1,0:T(8,128)S(1)} %join.5.near_ref), channel_id=1, source_target_pairs={{0,2},{1,3},{2,0},{3,1},{4,6},{5,7},{6,4},{7,5},{8,10},{9,11},{10,... | collective-permute-start | bytes 786440 | tf_op jit(solution)/shard_map/ppermute | solution.py:405
  102.0 2.0 %collective-permute-start.18 = (f32[512,256]{1,0:T(8,128)S(1)}, f32[512,256]{1,0:T(8,128)S(1)}, u32[]{:S(2)}, u32[]{:S(2)}) collective-permute-start(f32[512,256]{1,0:T(8,128)S(1)} %join.6.near_ref), channel_id=1, source_target_pairs={{0,1},{1,0},{2,3},{3,2},{4,5},{5,4},{6,7},{7,6},{8,9},{9,8},{10,11... | collective-permute-start | bytes 1572872 | tf_op jit(solution)/shard_map/ppermute | solution.py:405
  110.0 7.3 %collective-permute-start.19 = (f32[64,256]{1,0:T(8,128)}, f32[64,256]{1,0:T(8,128)S(1)}, u32[]{:S(2)}, u32[]{:S(2)}) collective-permute-start(f32[64,256]{1,0:T(8,128)} %copy-done.8), channel_id=1, source_target_pairs={{0,8},{1,9},{2,10},{3,11},{4,12},{5,13},{6,14},{7,15},{8,0},{9,1},... | collective-permute-start | bytes 196616 | tf_op jit(solution)/shard_map/ppermute | solution.py:405
  118.2 5.0 %collective-permute-start.20 = (f32[128,256]{1,0:T(8,128)S(1)}, f32[128,256]{1,0:T(8,128)S(1)}, u32[]{:S(2)}, u32[]{:S(2)}) collective-permute-start(f32[128,256]{1,0:T(8,128)S(1)} %join.7.near_ref), channel_id=1, source_target_pairs={{0,4},{1,5},{2,6},{3,7},{4,0},{5,1},{6,2},{7,3},{8,12},{9,13},{10,... | collective-permute-start | bytes 393224 | tf_op jit(solution)/shard_map/ppermute | solution.py:405
  123.2 7.2 %collective-permute-start.21 = (f32[256,256]{1,0:T(8,128)S(1)}, f32[256,256]{1,0:T(8,128)S(1)}, u32[]{:S(2)}, u32[]{:S(2)}) collective-permute-start(f32[256,256]{1,0:T(8,128)S(1)} %join.8.near_ref), channel_id=1, source_target_pairs={{0,2},{1,3},{2,0},{3,1},{4,6},{5,7},{6,4},{7,5},{8,10},{9,11},{10,... | collective-permute-start | bytes 786440 | tf_op jit(solution)/shard_map/ppermute | solution.py:405
  128.0 12.8 %collective-permute-start.22 = (f32[16,16,512]{2,1,0:T(8,128)}, f32[16,16,512]{2,1,0:T(8,128)S(1)}, u32[]{:S(2)}, u32[]{:S(2)}) collective-permute-start(f32[16,16,512]{2,1,0:T(8,128)} %all-to-all-done.first_ref), channel_id=1, source_target_pairs={{0,16},{16,0},{1,17},{17,1},{2,18},{18,2},{3,19},{19,3},{4,20},{20... | collective-permute-start | bytes 1572872 | tf_op jit(solution)/shard_map/ppermute | solution.py:470
  130.4 10.3 %collective-permute-start.23 = (f32[512,256]{1,0:T(8,128)S(1)}, f32[512,256]{1,0:T(8,128)S(1)}, u32[]{:S(2)}, u32[]{:S(2)}) collective-permute-start(f32[512,256]{1,0:T(8,128)S(1)} %join.9.refs_0_), channel_id=1, source_target_pairs={{0,1},{1,0},{2,3},{3,2},{4,5},{5,4},{6,7},{7,6},{8,9},{9,8},{10,11... | collective-permute-start | bytes 1572872 | tf_op jit(solution)/shard_map/ppermute | solution.py:405
  (16 other events, 145.9 us)

commit v3 on v2

--- a/solution.py
+++ b/solution.py
@@ -379,25 +379,44 @@
         in_specs=[SMEM, VMEM],
         out_specs=VMEM,
         name="turn_rows",
-        compiler_params=grant(8),
+        compiler_params=grant(60),
     )(turn, weight)
 
 
-def join_kernel(near_ref, far_ref, out_ref):
-    half = near_ref.shape[0]
-    out_ref[:half] = near_ref[...]
-    out_ref[half:] = far_ref[...]
-
-
-def join(near, far):
+def join_kernel(*refs):
+    size = refs[0].shape[0]
+    for at, piece in enumerate(refs[:-1]):
+        refs[-1][at * size : (at + 1) * size] = piece[...]
+
+
+def join(pieces):
+    size, cells = pieces[0].shape
     return pl.pallas_call(
         join_kernel,
-        out_shape=jax.ShapeDtypeStruct((2 * near.shape[0], near.shape[1]), jnp.float32),
-        in_specs=[VMEM] * 2,
+        out_shape=jax.ShapeDtypeStruct((len(pieces) * size, cells), jnp.float32),
+        in_specs=[VMEM] * len(pieces),
         out_specs=VMEM,
         name="join",
         compiler_params=grant(4),
-    )(near, far)
+    )(*pieces)
+
+
+def scatter(held, bits):
+    parts = jnp.split(held, 1 << len(bits), axis=0)
+    offsets = [0]
+    for bit in bits[::-1]:
+        offsets += [offset ^ bit for offset in offsets]
+    total = parts[0]
+    for part, offset in list(zip(parts, offsets))[1:]:
+        total = total + swap(part, offset)
+    return total
+
+
+def gather(held, bits):
+    offsets = [0]
+    for bit in bits[::-1]:
+        offsets += [offset ^ bit for offset in offsets]
+    return join([held] + [swap(held, offset) for offset in offsets[1:]])
 
 
 def swap(field, bit):
@@ -416,12 +435,13 @@
     place_fine = jnp.asarray(picker(1, YA, ZA, np).T)
     pick_mid = picker(PACK, MID_ROWS, MID_COLS)
 
+    turn_array = (lax.axis_index("groups") % 2).astype(jnp.int32).reshape(1)
+    w_half = turn_rows(turn_array, w_up_deep.reshape(8 * deep_local, chan_mid), count)
+    w_near = lax.all_to_all(w_half, "wide", split_axis=0, concat_axis=0, tiled=True)
     mid_input = down_fine(fine_field, place_fine, w_down_fine)
 
     conv_high, conv_low = split_outside(w_conv_mid.reshape(27 * mid_local, chan_mid))
     down_weight = w_down_mid.reshape(8 * mid_local, chan_deep)
-    turn_array = (lax.axis_index("groups") % 2).astype(jnp.int32).reshape(1)
-    w_half = turn_rows(turn_array, w_up_deep.reshape(8 * deep_local, chan_mid), count)
 
     ring = list(range(0, chips, 2)) + list(range(chips - 1, 0, -2))
     links = [(2 * ring[k], 2 * ring[(k + 1) % chips]) for k in range(chips)]
@@ -453,27 +473,23 @@
 
     deep_high, deep_low = split_outside(w_conv_deep.reshape(27 * deep_local, chan_deep))
     held = keep + swap(send, 1)
-    for bit in bits[1:-1]:
-        size = held.shape[0] // 2
-        held = held[:size] + swap(held[size:], bit)
-        if bit == bits[1]:
-            held, deep_high, deep_low = lax.optimization_barrier((held, deep_high, deep_low))
-    held = jax.nn.relu(held + swap(held, bits[-1]))
-    held, w_half = lax.optimization_barrier((held, w_half))
-    for bit in bits[-2:0:-1]:
-        held = join(held, swap(held, bit))
-    w_near = lax.all_to_all(w_half, "wide", split_axis=0, concat_axis=0, tiled=True)
-    deep_output = conv_deep(me_array, count // 2, deep_high, deep_low, held, swap(held, 1))
-
-    deep_output, w_near = lax.optimization_barrier((deep_output, w_near))
+    groups = [bits[at : min(at + 2, len(bits) - 1)] for at in range(1, len(bits) - 1, 2)]
+    for group in groups:
+        held = scatter(held, group)
+    held, w_near = lax.optimization_barrier((held, w_near))
     pairs = [(i, i ^ 1) for i in range(lax.axis_size("groups"))]
     w_far = lax.ppermute(w_near, "groups", pairs)
+    held = jax.nn.relu(held + swap(held, bits[-1]))
+    held, deep_high, deep_low = lax.optimization_barrier((held, deep_high, deep_low))
+    for group in groups[::-1]:
+        held = gather(held, group)
+    deep_output = conv_deep(me_array, count // 2, deep_high, deep_low, held, swap(held, 1))
+
     last_high, last_low = split_outside(w_up_mid)
-    held = deep_output
-    for bit in bits[:0:-1]:
-        held = join(held, swap(held, bit))
-        if bit == bits[1]:
-            held, last_high, last_low = lax.optimization_barrier((held, last_high, last_low))
+    held = gather(deep_output, bits[-1:])
+    for group in groups[::-1]:
+        held = gather(held, group)
+    held, last_high, last_low = lax.optimization_barrier((held, last_high, last_low))
     other = swap(held, 1)
     merged = up_deep(me_array, turn_array, count, w_near, w_far, held, other, pick_mid.T, mid_field)
 

time: 159 us -> 138 us (0.87)
  waiting for transfers between devices: 67.3 us -> 55.6 us
  local copies, waits for them, and re-layouts: 6.46 us -> 0.05 us
  other arithmetic: 9.96 us -> 6.07 us
    ppermute x16 -> x19, waiting for transfers between devices: 40.9 us -> 31.5 us  [swap(): return lax.ppermute(field, 'wide', [(i, i ^ bit) for i in range(count)])]
    unnamed x30 -> x10, local copies, waits for them, and re-layouts: 6.43 us -> 0.02 us
    ppermute x1, waiting for transfers between devices: 10.2 us -> 7.86 us  [shards(): w_far = lax.ppermute(w_near, 'groups', pairs)]
    pallas_call x1, Pallas kernels: 0.32 us -> 2.35 us  [turn_rows(): pl.pallas_call(turn_rows_kernel, out_shape=jax.ShapeDtypeStruct((count, c...]
    max x1, other arithmetic: 1.65 us -> 0.02 us  [shards(): held = jax.nn.relu(held + swap(held, bits[-1]))]
    ppermute x16 -> x19, starting transfers between devices: 16.3 us -> 16.1 us  [swap(): return lax.ppermute(field, 'wide', [(i, i ^ bit) for i in range(count)])]
  transfers between devices with their start and end apart: 25 -> 28, of which waited for: 19 -> 19; matrix products, arithmetic and copies ran while one was open for 5% -> 4% of each run, Pallas kernels for 4% -> 3%
where the time goes in v3:
time: 138 us
  waiting for transfers between devices  55.6 us (40%)
  starting transfers between devices  37.6 us (27%)
  Pallas kernels  25.5 us (18%)
  blocking collectives  12.9 us (9%)
  other arithmetic  6.07 us (4%)
    ppermute x19, waiting for transfers between devices, swap(): return lax.ppermute(field, 'wide', [(i, i ^ bit) for i in range(count)])  31.5 us
    ppermute x19, starting transfers between devices, swap(): return lax.ppermute(field, 'wide', [(i, i ^ bit) for i in range(count)])  16.1 us
    all_to_all x1, blocking collectives, shards(): lax.all_to_all(merged, 'wide', split_axis=0, concat_axis=0, tiled=True)  12.9 us
    ppermute x4, waiting for transfers between devices, shards(): near = lax.ppermute(near, 'wide', links)  9.83 us
    ppermute x4, starting transfers between devices, shards(): near = lax.ppermute(near, 'wide', links)  8.68 us
    ppermute x1, waiting for transfers between devices, shards(): w_far = lax.ppermute(w_near, 'groups', pairs)  7.86 us
    pallas_call x1, Pallas kernels, down_fine(): pl.pallas_call(down_fine_kernel, out_shape=jax.ShapeDtypeStruct((chan_mid...  7.61 us
    ppermute x3, waiting for transfers between devices, shards(): far = lax.ppermute(far, 'wide', links)  6.42 us
  transfers between devices with their start and end apart: 28, of which 19 were waited for; matrix products, arithmetic and copies ran while one was open for 4% of the time, Pallas kernels for 3%

profile of v3, /device:TPU:0, one launch (start us, length us, event | category | flops | bytes accessed | tf_op | source)
XLA Modules:
  0.0 138.0 jit_solution(3980949764642927893)
XLA Ops:
  0.0 7.6 %down_fine.1.refs_0_ = f32[512,128]{1,0:T(8,128)} custom-call(f32[256,2,512]{2,1,0:T(2,128)} %field_ref.1, bf16[512,512]{1,0:T(8,128)(2,1)} %constant.111.clone.place_ref, f32[8,256,512]{2,1,0:T(8,128)} %weight_ref.1), custom_call_target="tpu_custom_call" | custom-call | tf_op jit(solution)/shard_map/down_fine/pallas_call | solution.py:97
  8.1 2.6 %collective-permute-start = (f32[512,128]{1,0:T(8,128)}, f32[512,128]{1,0:T(8,128)S(1)}, u32[]{:S(2)}, u32[]{:S(2)}) collective-permute-start(f32[512,128]{1,0:T(8,128)} %down_fine.1.refs_0_), channel_id=1, source_target_pairs={{0,4},{4,8},{8,12},{12,14},{14,10},{10,6},{6,2},{2,0},{5,1},{9,5},... | collective-permute-start | bytes 786440 | tf_op jit(solution)/shard_map/ppermute | solution.py:454
  12.7 2.6 %collective-permute-done.refs_2_ = f32[512,128]{1,0:T(8,128)S(1)} collective-permute-done((f32[512,128]{1,0:T(8,128)}, f32[512,128]{1,0:T(8,128)S(1)}, u32[]{:S(2)}, u32[]{:S(2)}) %collective-permute-start) | collective-permute-done | bytes 262176 | tf_op jit(solution)/shard_map/ppermute | solution.py:454
  15.2 2.8 %collective-permute-done.2.refs_3_ = f32[512,128]{1,0:T(8,128)S(1)} collective-permute-done((f32[512,128]{1,0:T(8,128)S(1)}, f32[512,128]{1,0:T(8,128)S(1)}, u32[]{:S(2)}, u32[]{:S(2)}) %collective-permute-start.2) | collective-permute-done | bytes 262176 | tf_op jit(solution)/shard_map/ppermute | solution.py:456
  19.9 2.1 %collective-permute-start.4 = (f32[512,128]{1,0:T(8,128)S(1)}, f32[512,128]{1,0:T(8,128)S(1)}, u32[]{:S(2)}, u32[]{:S(2)}) collective-permute-start(f32[512,128]{1,0:T(8,128)S(1)} %collective-permute-done.refs_2_), channel_id=1, source_target_pairs={{0,4},{4,8},{8,12},{12,14},{14,10},{10,6},{6,2},{2,0},{5,1},{9,5},... | collective-permute-start | bytes 786440 | tf_op jit(solution)/shard_map/ppermute | solution.py:454
  23.5 2.8 %collective-permute-done.4.refs_1_ = f32[512,128]{1,0:T(8,128)S(1)} collective-permute-done((f32[512,128]{1,0:T(8,128)S(1)}, f32[512,128]{1,0:T(8,128)S(1)}, u32[]{:S(2)}, u32[]{:S(2)}) %collective-permute-start.4) | collective-permute-done | bytes 262176 | tf_op jit(solution)/shard_map/ppermute | solution.py:454
  26.3 2.8 %collective-permute-done.5.refs_2_ = f32[512,128]{1,0:T(8,128)S(1)} collective-permute-done((f32[512,128]{1,0:T(8,128)S(1)}, f32[512,128]{1,0:T(8,128)S(1)}, u32[]{:S(2)}, u32[]{:S(2)}) %collective-permute-start.5) | collective-permute-done | bytes 262176 | tf_op jit(solution)/shard_map/ppermute | solution.py:456
  31.0 2.1 %collective-permute-start.7 = (f32[512,128]{1,0:T(8,128)S(1)}, f32[512,128]{1,0:T(8,128)S(1)}, u32[]{:S(2)}, u32[]{:S(2)}) collective-permute-start(f32[512,128]{1,0:T(8,128)S(1)} %collective-permute-done.4.refs_1_), channel_id=1, source_target_pairs={{0,4},{4,8},{8,12},{12,14},{14,10},{10,6},{6,2},{2,0},{5,1},{9,5},... | collective-permute-start | bytes 786440 | tf_op jit(solution)/shard_map/ppermute | solution.py:454
  34.7 2.8 %collective-permute-done.7.refs_1_ = f32[512,128]{1,0:T(8,128)S(1)} collective-permute-done((f32[512,128]{1,0:T(8,128)S(1)}, f32[512,128]{1,0:T(8,128)S(1)}, u32[]{:S(2)}, u32[]{:S(2)}) %collective-permute-start.7) | collective-permute-done | bytes 262176 | tf_op jit(solution)/shard_map/ppermute | solution.py:454
  45.4 2.6 %down_mid.1 = (f32[16,32,128]{2,1,0:T(8,128)S(1)}, f32[512,256]{1,0:T(8,128)S(1)}, f32[512,256]{1,0:T(8,128)S(1)}) custom-call(s32[1]{0:T(128)} %bitcast.me_ref, bf16[864,512]{1,0:T(8,128)(2,1)S(1)} %get-tuple-element.31.high_ref, bf16[864,512]{1,0:T(8,128)(2,1)S(1)} %get-tuple-element.32.low_ref, bf16[512,512]{1,0:T(8,128)(2,1)S(1)} %get-tuple-element.67.pick_ref, ...), custom_call_target="tpu_custom_call" | custom-call | tf_op jit(solution)/shard_map/down_mid/pallas_call | solution.py:221
  48.2 2.4 %turn_rows.1 = f32[16,16,512]{2,1,0:T(8,128)} custom-call(s32[1]{0:T(128)} %bitcast.3.turn_ref, f32[512,512]{1,0:T(8,128)} %bitcast.11), custom_call_target="tpu_custom_call" | custom-call | tf_op jit(solution)/shard_map/turn_rows/pallas_call | solution.py:376
  50.6 6.4 %all-to-all-start = ((f32[16,16,512]{2,1,0:T(8,128)}), f32[16,16,512]{2,1,0:T(8,128)S(1)}, u32[]{:S(2)}, u32[]{:S(2)}) async-start(f32[16,16,512]{2,1,0:T(8,128)} %turn_rows.1), calls=%async_computation | async-start | bytes 1048576 | tf_op jit(solution)/shard_map/all_to_all | solution.py:440
  60.7 11.2 %collective-permute-done.13 = f32[128,256]{1,0:T(8,128)S(1)} collective-permute-done((f32[128,256]{1,0:T(8,128)S(1)}, f32[128,256]{1,0:T(8,128)S(1)}, u32[]{:S(2)}, u32[]{:S(2)}) %collective-permute-start.13) | collective-permute-done | bytes 131104 | tf_op jit(solution)/shard_map/ppermute | solution.py:424
  71.9 3.1 %collective-permute-done.15 = f32[128,256]{1,0:T(8,128)S(1)} collective-permute-done((f32[128,256]{1,0:T(8,128)S(1)}, f32[128,256]{1,0:T(8,128)S(1)}, u32[]{:S(2)}, u32[]{:S(2)}) %collective-permute-start.15) | collective-permute-done | bytes 131104 | tf_op jit(solution)/shard_map/ppermute | solution.py:424
  75.1 2.5 %collective-permute-start.16 = (f32[128,256]{1,0:T(8,128)S(1)}, f32[128,256]{1,0:T(8,128)S(1)}, u32[]{:S(2)}, u32[]{:S(2)}) collective-permute-start(f32[128,256]{1,0:T(8,128)S(1)} %fusion.6), channel_id=1, source_target_pairs={{0,8},{1,9},{2,10},{3,11},{4,12},{5,13},{6,14},{7,15},{8,0},{9,1},... | collective-permute-start | bytes 393224 | tf_op jit(solution)/shard_map/ppermute | solution.py:424
  77.5 4.6 %fusion = (bf16[1728,1024]{1,0:T(8,128)(2,1)S(1)}, bf16[1728,1024]{1,0:T(8,128)(2,1)S(1)}) fusion(f32[27,64,1024]{2,1,0:T(8,128)} %param.12), kind=kLoop, calls=%fused_computation.2 | loop fusion | flops 7077888 | bytes 14155776 | tf_op jit(solution)/shard_map/convert_element_type | solution.py:30
  84.5 2.8 %collective-permute-start.19 = (f32[128,256]{1,0:T(8,128)S(1)}, f32[128,256]{1,0:T(8,128)S(1)}, u32[]{:S(2)}, u32[]{:S(2)}) collective-permute-start(f32[128,256]{1,0:T(8,128)S(1)} %add_maximum_fusion.refs_0_), channel_id=1, source_target_pairs={{0,6},{1,7},{2,4},{3,5},{4,2},{5,3},{6,0},{7,1},{8,14},{9,15},{10,... | collective-permute-start | bytes 393224 | tf_op jit(solution)/shard_map/ppermute | solution.py:424
  87.4 2.9 %collective-permute-done.17.refs_1_ = f32[128,256]{1,0:T(8,128)S(1)} collective-permute-done((f32[128,256]{1,0:T(8,128)S(1)}, f32[128,256]{1,0:T(8,128)S(1)}, u32[]{:S(2)}, u32[]{:S(2)}) %collective-permute-start.17) | collective-permute-done | bytes 131104 | tf_op jit(solution)/shard_map/ppermute | solution.py:424
  94.2 3.4 %conv_deep.1.refs_0_ = f32[64,256]{1,0:T(8,128)S(1)} custom-call(s32[1]{0:T(128)} %bitcast.me_ref, bf16[1728,1024]{1,0:T(8,128)(2,1)S(1)} %get-tuple-element.49.high_ref, bf16[1728,1024]{1,0:T(8,128)(2,1)S(1)} %get-tuple-element.50.low_ref, f32[512,256]{1,0:T(8,128)S(1)} %join.3.near_ref, f32[512,256]{1,0:T(8,128)S(1)} %collective-permute-done.20.far_ref), custom_call_target="tpu_custom_call" | custom-call | tf_op jit(solution)/shard_map/conv_deep/pallas_call | solution.py:281
  99.5 4.7 %collective-permute-done.21.refs_1_ = f32[64,256]{1,0:T(8,128)S(1)} collective-permute-done((f32[64,256]{1,0:T(8,128)S(1)}, f32[64,256]{1,0:T(8,128)S(1)}, u32[]{:S(2)}, u32[]{:S(2)}) %collective-permute-start.21) | collective-permute-done | bytes 65568 | tf_op jit(solution)/shard_map/ppermute | solution.py:424
  105.6 2.2 %collective-permute-start.24 = (f32[128,256]{1,0:T(8,128)S(1)}, f32[128,256]{1,0:T(8,128)S(1)}, u32[]{:S(2)}, u32[]{:S(2)}) collective-permute-start(f32[128,256]{1,0:T(8,128)S(1)} %join.4.refs_0_), channel_id=1, source_target_pairs={{0,6},{1,7},{2,4},{3,5},{4,2},{5,3},{6,0},{7,1},{8,14},{9,15},{10,... | collective-permute-start | bytes 393224 | tf_op jit(solution)/shard_map/ppermute | solution.py:424
  113.1 7.9 %collective-permute-done.25.second_ref = f32[16,16,512]{2,1,0:T(8,128)S(1)} collective-permute-done((f32[16,16,512]{2,1,0:T(8,128)S(1)}, f32[16,16,512]{2,1,0:T(8,128)S(1)}, u32[]{:S(2)}, u32[]{:S(2)}) %collective-permute-start.25) | collective-permute-done | bytes 524320 | tf_op jit(solution)/shard_map/ppermute | solution.py:481
  122.2 12.9 %all_to_all.10.field_ref = f32[16,32,128]{2,1,0:T(8,128)S(1)} all-to-all(f32[16,32,128]{2,1,0:T(8,128)S(1)} %up_deep.1), channel_id=1, replica_groups=mesh['groups'=2,'wide'=16] {'wide'}, dimensions={0} | all-to-all | bytes 524288 | tf_op jit(solution)/shard_map/all_to_all | solution.py:496
  135.1 2.8 %up_mid.1 = f32[256,2,512]{2,1,0:T(2,128)} custom-call(bf16[8,512,256]{2,1,0:T(8,128)(2,1)S(1)} %get-tuple-element.52.high_ref, bf16[8,512,256]{2,1,0:T(8,128)(2,1)S(1)} %get-tuple-element.53.low_ref, f32[16,32,128]{2,1,0:T(8,128)S(1)} %all_to_all.10.field_ref, bf16[512,512]{1,0:T(8,128)(2,1)S(1)} %copy-done), custom_call_target="tpu_custom_call" | custom-call | tf_op jit(solution)/shard_map/up_mid/pallas_call | solution.py:358
  (64 shorter events, 37.3 us)
Async XLA Ops:
  8.1 7.1 %collective-permute-start = (f32[512,128]{1,0:T(8,128)}, f32[512,128]{1,0:T(8,128)S(1)}, u32[]{:S(2)}, u32[]{:S(2)}) collective-permute-start(f32[512,128]{1,0:T(8,128)} %down_fine.1.refs_0_), channel_id=1, source_target_pairs={{0,4},{4,8},{8,12},{12,14},{14,10},{10,6},{6,2},{2,0},{5,1},{9,5},... | collective-permute-start | bytes 786440 | tf_op jit(solution)/shard_map/ppermute | solution.py:454
  10.7 7.4 %collective-permute-start.2 = (f32[512,128]{1,0:T(8,128)S(1)}, f32[512,128]{1,0:T(8,128)S(1)}, u32[]{:S(2)}, u32[]{:S(2)}) collective-permute-start(f32[512,128]{1,0:T(8,128)S(1)} %collective-permute-done.1.refs_1_), channel_id=1, source_target_pairs={{0,4},{4,8},{8,12},{12,14},{14,10},{10,6},{6,2},{2,0},{5,1},{9,5},... | collective-permute-start | bytes 786440 | tf_op jit(solution)/shard_map/ppermute | solution.py:456
  19.8 9.3 %collective-permute-start.3 = (f32[512,256]{1,0:T(8,128)S(1)}, f32[512,256]{1,0:T(8,128)S(1)}, u32[]{:S(2)}, u32[]{:S(2)}) collective-permute-start(f32[512,256]{1,0:T(8,128)S(1)} %get-tuple-element.34), channel_id=1, source_target_pairs={{0,1},{1,0},{2,3},{3,2},{4,5},{5,4},{6,7},{7,6},{8,9},{9,8},{10,11... | collective-permute-start | bytes 1572872 | tf_op jit(solution)/shard_map/ppermute | solution.py:424
  19.9 6.4 %collective-permute-start.4 = (f32[512,128]{1,0:T(8,128)S(1)}, f32[512,128]{1,0:T(8,128)S(1)}, u32[]{:S(2)}, u32[]{:S(2)}) collective-permute-start(f32[512,128]{1,0:T(8,128)S(1)} %collective-permute-done.refs_2_), channel_id=1, source_target_pairs={{0,4},{4,8},{8,12},{12,14},{14,10},{10,6},{6,2},{2,0},{5,1},{9,5},... | collective-permute-start | bytes 786440 | tf_op jit(solution)/shard_map/ppermute | solution.py:454
  22.0 7.2 %collective-permute-start.5 = (f32[512,128]{1,0:T(8,128)S(1)}, f32[512,128]{1,0:T(8,128)S(1)}, u32[]{:S(2)}, u32[]{:S(2)}) collective-permute-start(f32[512,128]{1,0:T(8,128)S(1)} %collective-permute-done.2.refs_3_), channel_id=1, source_target_pairs={{0,4},{4,8},{8,12},{12,14},{14,10},{10,6},{6,2},{2,0},{5,1},{9,5},... | collective-permute-start | bytes 786440 | tf_op jit(solution)/shard_map/ppermute | solution.py:456
  31.0 9.3 %collective-permute-start.6 = (f32[512,256]{1,0:T(8,128)S(1)}, f32[512,256]{1,0:T(8,128)S(1)}, u32[]{:S(2)}, u32[]{:S(2)}) collective-permute-start(f32[512,256]{1,0:T(8,128)S(1)} %get-tuple-element.38), channel_id=1, source_target_pairs={{0,1},{1,0},{2,3},{3,2},{4,5},{5,4},{6,7},{7,6},{8,9},{9,8},{10,11... | collective-permute-start | bytes 1572872 | tf_op jit(solution)/shard_map/ppermute | solution.py:424
  31.0 6.4 %collective-permute-start.7 = (f32[512,128]{1,0:T(8,128)S(1)}, f32[512,128]{1,0:T(8,128)S(1)}, u32[]{:S(2)}, u32[]{:S(2)}) collective-permute-start(f32[512,128]{1,0:T(8,128)S(1)} %collective-permute-done.4.refs_1_), channel_id=1, source_target_pairs={{0,4},{4,8},{8,12},{12,14},{14,10},{10,6},{6,2},{2,0},{5,1},{9,5},... | collective-permute-start | bytes 786440 | tf_op jit(solution)/shard_map/ppermute | solution.py:454
  33.1 7.2 %collective-permute-start.8 = (f32[512,128]{1,0:T(8,128)S(1)}, f32[512,128]{1,0:T(8,128)S(1)}, u32[]{:S(2)}, u32[]{:S(2)}) collective-permute-start(f32[512,128]{1,0:T(8,128)S(1)} %collective-permute-done.5.refs_2_), channel_id=1, source_target_pairs={{0,4},{4,8},{8,12},{12,14},{14,10},{10,6},{6,2},{2,0},{5,1},{9,5},... | collective-permute-start | bytes 786440 | tf_op jit(solution)/shard_map/ppermute | solution.py:456
  37.5 6.4 %collective-permute-start.10 = (f32[512,128]{1,0:T(8,128)S(1)}, f32[512,128]{1,0:T(8,128)S(1)}, u32[]{:S(2)}, u32[]{:S(2)}) collective-permute-start(f32[512,128]{1,0:T(8,128)S(1)} %collective-permute-done.7.refs_1_), channel_id=1, source_target_pairs={{0,4},{4,8},{8,12},{12,14},{14,10},{10,6},{6,2},{2,0},{5,1},{9,5},... | collective-permute-start | bytes 786440 | tf_op jit(solution)/shard_map/ppermute | solution.py:454
  48.0 8.9 %collective-permute-start.12 = (f32[512,256]{1,0:T(8,128)S(1)}, f32[512,256]{1,0:T(8,128)S(1)}, u32[]{:S(2)}, u32[]{:S(2)}) collective-permute-start(f32[512,256]{1,0:T(8,128)S(1)} %get-tuple-element.47), channel_id=1, source_target_pairs={{0,1},{1,0},{2,3},{3,2},{4,5},{5,4},{6,7},{7,6},{8,9},{9,8},{10,11... | collective-permute-start | bytes 1572872 | tf_op jit(solution)/shard_map/ppermute | solution.py:424
  50.6 24.5 %all-to-all-start = ((f32[16,16,512]{2,1,0:T(8,128)}), f32[16,16,512]{2,1,0:T(8,128)S(1)}, u32[]{:S(2)}, u32[]{:S(2)}) async-start(f32[16,16,512]{2,1,0:T(8,128)} %turn_rows.1), calls=%async_computation | async-start | bytes 1048576 | tf_op jit(solution)/shard_map/all_to_all | solution.py:440
  57.1 14.8 %collective-permute-start.13 = (f32[128,256]{1,0:T(8,128)S(1)}, f32[128,256]{1,0:T(8,128)S(1)}, u32[]{:S(2)}, u32[]{:S(2)}) collective-permute-start(f32[128,256]{1,0:T(8,128)S(1)} %get-tuple-element.63), channel_id=1, source_target_pairs={{0,4},{1,5},{2,6},{3,7},{4,0},{5,1},{6,2},{7,3},{8,12},{9,13},{10,... | collective-permute-start | bytes 393224 | tf_op jit(solution)/shard_map/ppermute | solution.py:424
  59.1 12.8 %collective-permute-start.14 = (f32[128,256]{1,0:T(8,128)S(1)}, f32[128,256]{1,0:T(8,128)S(1)}, u32[]{:S(2)}, u32[]{:S(2)}) collective-permute-start(f32[128,256]{1,0:T(8,128)S(1)} %get-tuple-element.65), channel_id=1, source_target_pairs={{0,2},{1,3},{2,0},{3,1},{4,6},{5,7},{6,4},{7,5},{8,10},{9,11},{10,... | collective-permute-start | bytes 393224 | tf_op jit(solution)/shard_map/ppermute | solution.py:424
  60.5 14.5 %collective-permute-start.15 = (f32[128,256]{1,0:T(8,128)S(1)}, f32[128,256]{1,0:T(8,128)S(1)}, u32[]{:S(2)}, u32[]{:S(2)}) collective-permute-start(f32[128,256]{1,0:T(8,128)S(1)} %get-tuple-element.64), channel_id=1, source_target_pairs={{0,6},{1,7},{2,4},{3,5},{4,2},{5,3},{6,0},{7,1},{8,14},{9,15},{10,... | collective-permute-start | bytes 393224 | tf_op jit(solution)/shard_map/ppermute | solution.py:424
  75.1 8.7 %collective-permute-start.16 = (f32[128,256]{1,0:T(8,128)S(1)}, f32[128,256]{1,0:T(8,128)S(1)}, u32[]{:S(2)}, u32[]{:S(2)}) collective-permute-start(f32[128,256]{1,0:T(8,128)S(1)} %fusion.6), channel_id=1, source_target_pairs={{0,8},{1,9},{2,10},{3,11},{4,12},{5,13},{6,14},{7,15},{8,0},{9,1},... | collective-permute-start | bytes 393224 | tf_op jit(solution)/shard_map/ppermute | solution.py:424
  83.8 6.4 %collective-permute-start.17 = (f32[128,256]{1,0:T(8,128)S(1)}, f32[128,256]{1,0:T(8,128)S(1)}, u32[]{:S(2)}, u32[]{:S(2)}) collective-permute-start(f32[128,256]{1,0:T(8,128)S(1)} %add_maximum_fusion.refs_0_), channel_id=1, source_target_pairs={{0,4},{1,5},{2,6},{3,7},{4,0},{5,1},{6,2},{7,3},{8,12},{9,13},{10,... | collective-permute-start | bytes 393224 | tf_op jit(solution)/shard_map/ppermute | solution.py:424
  83.9 8.2 %collective-permute-start.18 = (f32[128,256]{1,0:T(8,128)S(1)}, f32[128,256]{1,0:T(8,128)S(1)}, u32[]{:S(2)}, u32[]{:S(2)}) collective-permute-start(f32[128,256]{1,0:T(8,128)S(1)} %add_maximum_fusion.refs_0_), channel_id=1, source_target_pairs={{0,2},{1,3},{2,0},{3,1},{4,6},{5,7},{6,4},{7,5},{8,10},{9,11},{10,... | collective-permute-start | bytes 393224 | tf_op jit(solution)/shard_map/ppermute | solution.py:424
  84.5 7.6 %collective-permute-start.19 = (f32[128,256]{1,0:T(8,128)S(1)}, f32[128,256]{1,0:T(8,128)S(1)}, u32[]{:S(2)}, u32[]{:S(2)}) collective-permute-start(f32[128,256]{1,0:T(8,128)S(1)} %add_maximum_fusion.refs_0_), channel_id=1, source_target_pairs={{0,6},{1,7},{2,4},{3,5},{4,2},{5,3},{6,0},{7,1},{8,14},{9,15},{10,... | collective-permute-start | bytes 393224 | tf_op jit(solution)/shard_map/ppermute | solution.py:424
  97.5 6.6 %collective-permute-start.21 = (f32[64,256]{1,0:T(8,128)S(1)}, f32[64,256]{1,0:T(8,128)S(1)}, u32[]{:S(2)}, u32[]{:S(2)}) collective-permute-start(f32[64,256]{1,0:T(8,128)S(1)} %conv_deep.1.refs_0_), channel_id=1, source_target_pairs={{0,8},{1,9},{2,10},{3,11},{4,12},{5,13},{6,14},{7,15},{8,0},{9,1},... | collective-permute-start | bytes 196616 | tf_op jit(solution)/shard_map/ppermute | solution.py:424
  104.2 6.3 %collective-permute-start.22 = (f32[128,256]{1,0:T(8,128)S(1)}, f32[128,256]{1,0:T(8,128)S(1)}, u32[]{:S(2)}, u32[]{:S(2)}) collective-permute-start(f32[128,256]{1,0:T(8,128)S(1)} %join.4.refs_0_), channel_id=1, source_target_pairs={{0,4},{1,5},{2,6},{3,7},{4,0},{5,1},{6,2},{7,3},{8,12},{9,13},{10,... | collective-permute-start | bytes 393224 | tf_op jit(solution)/shard_map/ppermute | solution.py:424
  104.5 6.7 %collective-permute-start.23 = (f32[128,256]{1,0:T(8,128)S(1)}, f32[128,256]{1,0:T(8,128)S(1)}, u32[]{:S(2)}, u32[]{:S(2)}) collective-permute-start(f32[128,256]{1,0:T(8,128)S(1)} %join.4.refs_0_), channel_id=1, source_target_pairs={{0,2},{1,3},{2,0},{3,1},{4,6},{5,7},{6,4},{7,5},{8,10},{9,11},{10,... | collective-permute-start | bytes 393224 | tf_op jit(solution)/shard_map/ppermute | solution.py:424
  105.6 7.4 %collective-permute-start.24 = (f32[128,256]{1,0:T(8,128)S(1)}, f32[128,256]{1,0:T(8,128)S(1)}, u32[]{:S(2)}, u32[]{:S(2)}) collective-permute-start(f32[128,256]{1,0:T(8,128)S(1)} %join.4.refs_0_), channel_id=1, source_target_pairs={{0,6},{1,7},{2,4},{3,5},{4,2},{5,3},{6,0},{7,1},{8,14},{9,15},{10,... | collective-permute-start | bytes 393224 | tf_op jit(solution)/shard_map/ppermute | solution.py:424
  108.6 12.4 %collective-permute-start.25 = (f32[16,16,512]{2,1,0:T(8,128)S(1)}, f32[16,16,512]{2,1,0:T(8,128)S(1)}, u32[]{:S(2)}, u32[]{:S(2)}) collective-permute-start(f32[16,16,512]{2,1,0:T(8,128)S(1)} %all-to-all-done.first_ref), channel_id=1, source_target_pairs={{0,16},{16,0},{1,17},{17,1},{2,18},{18,2},{3,19},{19,3},{4,20},{20... | collective-permute-start | bytes 1572872 | tf_op jit(solution)/shard_map/ppermute | solution.py:481
  113.0 7.9 %collective-permute-start.26 = (f32[512,256]{1,0:T(8,128)S(1)}, f32[512,256]{1,0:T(8,128)S(1)}, u32[]{:S(2)}, u32[]{:S(2)}) collective-permute-start(f32[512,256]{1,0:T(8,128)S(1)} %join.5.refs_0_), channel_id=1, source_target_pairs={{0,1},{1,0},{2,3},{3,2},{4,5},{5,4},{6,7},{7,6},{8,9},{9,8},{10,11... | collective-permute-start | bytes 1572872 | tf_op jit(solution)/shard_map/ppermute | solution.py:424
  (9 other events, 93.9 us)
